TPU v7x, 128 devices: a whole 4x4x4 slice. The times are simulated.
128 devices in a mesh: grp: 8 (over z_lo, x), obs: 16 (over y, z_hi, core).
Axes of the slice: x: 4, y: 4, z: 4 (z_hi: 2, z_lo: 2; z = z_hi * 2 + z_lo), core: 2. Of those that a mesh axis runs over, the one named last changes fastest.
Arguments:
- signals: bfloat16 [4, 256, 131072], P(None, None, ('grp', 'obs')), may hold values from -6 to 6
- patch_count: int32 [128], P(('grp', 'obs')), may hold values from 0 to 8, as said below
- patch_place: int32 [1024], P(('grp', 'obs')), may hold values from 0 to 63, as said below
- face_geom: float32 [4, 65536], P(None, ('grp', 'obs')), may hold values from -3.5 to 30, as said below
- obs_pos: float32 [3, 4096], P(None, 'obs'), may hold values from -60 to 60, as said below
Outputs:
- pressure: float32 [16, 4096], P('grp', 'obs')
Inputs may be any that keep to these rules, and one draw needn't show every extreme that they name: `patch_count`: each partition holds 0 to 8 live patches; in every face group the counts sum to 64 and some partition holds exactly 8. `patch_place`: A live slot names owner o and patch j of the partition's group as o * 4 + j; within a group every such value is named by exactly one live slot, so every owner receives exactly 4 patches; no partition holds two live patches of the same owner. Slots beyond the count hold arbitrary values in the range. `face_geom`: faces lie on a surface around the first coordinate's axis: the first coordinate between 0 and 30, the distance from that axis between 2 and 3.5; the area lies between 0.5 and 10. `obs_pos`: every observer lies 25 to 60 from the anchor (0, 0, 0) and 8 or more from the first coordinate's axis.
All inputs are finite; a program needn't handle non-finite values.
Results may differ from a plain program's by a relative error of at most 0.004.
Values may be sent and summed in bfloat16 or wider, within the bound.
No kernel may reach another device: no remote copies, remote signals or barrier semaphores. Data moves between devices by JAX's collectives and lax.ppermute only.
A program may use at most 64 MiB of HBM per device.

v0:
```python
import math

import jax
import jax.numpy as jnp
from jax import lax
from jax.sharding import PartitionSpec as P

SAMPLES = 256
NFREQ = 8
NSIG = 4
PATCH = 128
MAXP = 8
PER_OWN = 4
FACES_OWN = 512


omega_step = 0.5
four_pi = 4.0 * math.pi


def spectral_basis(samples, freq_count):
    sample_idx = jnp.arange(samples, dtype=jnp.float32)
    harmonic = jnp.arange(1, freq_count + 1, dtype=jnp.float32)
    angles = 2.0 * math.pi / samples * (sample_idx[:, None] * harmonic[None, :])
    window = (0.5 - 0.5 * jnp.cos(2.0 * math.pi / samples * sample_idx)) * math.sqrt(
        8.0 / (3.0 * samples)
    )
    table = jnp.concatenate(
        [window[:, None] * jnp.cos(angles), -window[:, None] * jnp.sin(angles)], axis=1
    )
    return table.astype(jnp.bfloat16)


def pressure_tiles(observers, spectra, geometry):
    freq_count = spectra.shape[0] // 8
    wavenumber = omega_step * jnp.arange(1, freq_count + 1, dtype=jnp.float32)
    values = spectra.reshape(4, 2, freq_count, spectra.shape[1])
    separation = observers[:, :, None] - geometry[:3, None, :]
    dist_sq = jnp.sum(separation * separation, axis=0)
    distance = jnp.sqrt(dist_sq)
    inv_sq = 1.0 / dist_sq
    load_re = jnp.zeros((freq_count,) + dist_sq.shape, jnp.float32)
    load_im = jnp.zeros((freq_count,) + dist_sq.shape, jnp.float32)
    for coord in range(3):
        load_re = load_re + values[1 + coord, 0][:, None, :] * separation[coord][None]
        load_im = load_im + values[1 + coord, 1][:, None, :] * separation[coord][None]
    dip_re = load_re * inv_sq[None]
    dip_im = load_im * inv_sq[None]
    omega_grid = wavenumber[:, None, None]
    phase = omega_grid * distance[None]
    mono_re = values[0, 0][:, None, :]
    mono_im = values[0, 1][:, None, :]
    bracket_re = -omega_grid * mono_im + dip_re - phase * dip_im
    bracket_im = omega_grid * mono_re + dip_im + phase * dip_re
    amplitude = (geometry[3][None, :] / (four_pi * distance))[None]
    green_re = amplitude * jnp.cos(phase)
    green_im = -amplitude * jnp.sin(phase)
    press_re = jnp.sum(green_re * bracket_re - green_im * bracket_im, axis=2)
    press_im = jnp.sum(green_re * bracket_im + green_im * bracket_re, axis=2)
    return jnp.concatenate([press_re, press_im], axis=0)


def accumulate(observers, spectra, geometry):
    face_count = spectra.shape[1]
    block_len = face_count
    while block_len > 128 and (
        block_len * observers.shape[1] > 131072 or face_count % block_len != 0
    ):
        block_len = block_len // 2
    step_count = face_count // block_len
    spec_blocks = spectra.reshape(spectra.shape[0], step_count, block_len).transpose(1, 0, 2)
    geom_blocks = geometry.reshape(4, step_count, block_len).transpose(1, 0, 2)

    def add_block(running, pieces):
        return (running + pressure_tiles(observers, pieces[0], pieces[1]), None)

    zero_sum = jnp.zeros((spectra.shape[0] // 4, observers.shape[1]), jnp.float32)
    result, _ = lax.scan(add_block, zero_sum, (spec_blocks, geom_blocks))
    return result


def local(signals, patch_count, patch_place, face_geom, obs_pos):
    owners = lax.axis_size("obs")
    channels = NSIG * 2 * NFREQ
    dft_basis = spectral_basis(SAMPLES, NFREQ).astype(jnp.float32)
    slot_index = jnp.arange(MAXP, dtype=jnp.int32)
    is_live = slot_index < patch_count[0]
    target_owner = patch_place // PER_OWN
    target_part = patch_place % PER_OWN
    owner_index = jnp.arange(owners, dtype=jnp.int32)
    picked = jnp.logical_and(target_owner[None, :] == owner_index[:, None], is_live[None, :])
    header = jnp.where(
        jnp.any(picked, axis=1), jnp.sum(jnp.where(picked, target_part[None, :], 0), axis=1), -1
    )
    select = picked.astype(jnp.bfloat16)
    row_blocks = signals.reshape(NSIG, SAMPLES, MAXP, PATCH)
    outgoing = jnp.einsum(
        "om,stmp->ostp", select, row_blocks, preferred_element_type=jnp.float32
    ).astype(jnp.bfloat16)
    arrived_rows, senders = (
        lax.all_to_all(outgoing, "obs", split_axis=0, concat_axis=0, tiled=True),
        lax.all_to_all(header, "obs", split_axis=0, concat_axis=0, tiled=True),
    )
    arrived = jnp.einsum(
        "ostp,tc->oscp",
        arrived_rows.astype(jnp.float32),
        dft_basis,
        precision=lax.Precision.HIGHEST,
    ).astype(jnp.bfloat16)
    arrived = arrived.reshape(owners, channels, PATCH)
    owned_part = (senders[:, None] == jnp.arange(PER_OWN, dtype=jnp.int32)[None, :]).astype(
        jnp.bfloat16
    )
    face_spec = jnp.einsum(
        "oj,okp->kjp", owned_part, arrived, preferred_element_type=jnp.float32
    ).astype(jnp.bfloat16)
    face_spec = face_spec.reshape(channels, FACES_OWN)
    spec_wide = face_spec.astype(jnp.float32)
    pressure = accumulate(
        obs_pos,
        lax.all_gather(spec_wide, "obs", axis=1, tiled=True),
        lax.all_gather(face_geom, "obs", axis=1, tiled=True),
    )
    rows_out = 2 * NFREQ // lax.axis_size("grp")
    summed = lax.psum(pressure, "grp")
    return lax.dynamic_slice_in_dim(summed, lax.axis_index("grp") * rows_out, rows_out, 0)


def solution(mesh):
    return jax.shard_map(
        local,
        mesh=mesh,
        in_specs=(
            P(None, None, ("grp", "obs")),
            P(("grp", "obs")),
            P(("grp", "obs")),
            P(None, ("grp", "obs")),
            P(None, "obs"),
        ),
        out_specs=P("grp", "obs"),
        check_vma=False,
    )
```

profile of v0, /device:TPU:1, one launch (start us, length us, event | category | flops | bytes accessed | tf_op | source)
XLA Modules:
  0.0 530.9 jit_solution(8264392097134709399)
XLA Ops:
  8.7 9.3 %all-to-all-start.1 = ((s32[16,1,1]{2,1,0:T(1,128)}), s32[16,1,1]{2,1,0:T(1,128)S(1)}, u32[]{:S(2)}, u32[]{:S(2)}) async-start(s32[16,1,1]{2,1,0:T(1,128)} %copy.22), calls=%async_computation.1 | async-start | bytes 16384 | tf_op jit(solution)/shard_map/all_to_all | solution.py:102
  25.0 6.8 %all-to-all-start = ((bf16[16,4,256,128]{3,2,1,0:T(8,128)(2,1)}), bf16[16,4,256,128]{3,2,1,0:T(8,128)(2,1)}, u32[]{:S(2)}, u32[]{:S(2)}) async-start(bf16[16,4,256,128]{3,2,1,0:T(8,128)(2,1)} %copy.21), calls=%async_computation | async-start | bytes 8388608 | tf_op jit(solution)/shard_map/all_to_all | solution.py:101
  32.5 52.5 %all-to-all-done = bf16[16,4,256,128]{3,2,1,0:T(8,128)(2,1)} async-done(((bf16[16,4,256,128]{3,2,1,0:T(8,128)(2,1)}), bf16[16,4,256,128]{3,2,1,0:T(8,128)(2,1)}, u32[]{:S(2)}, u32[]{:S(2)}) %all-to-all-start) | async-done | bytes 4194336 | tf_op jit(solution)/shard_map/all_to_all | solution.py:101
  88.8 29.2 %all_gather.6 = f32[4,8192]{1,0:T(4,128)S(1)} all-gather(f32[4,512]{1,0:T(4,128)S(1)} %copy-done.1), channel_id=1, replica_groups=mesh['grp'=8,'obs'=16] {'obs'}, dimensions={1}, use_global_device_ids=true | all-gather | bytes 139264 | tf_op jit(solution)/shard_map/all_gather | solution.py:122
  118.0 27.0 %all-gather.2.cloned.1.call-done = f32[64,8192]{1,0:T(8,128)} async-done(((f32[64,512]{1,0:T(8,128)}), f32[64,8192]{1,0:T(8,128)}) %all-gather.2.cloned.1.call-update) | async-done | bytes 2097168 | tf_op jit(solution)/shard_map/all_gather | solution.py:121
  145.0 4.1 copy.30
  149.1 348.0 %while.11 = (s32[]{:T(128)}, f32[16,256]{1,0:T(8,128)S(1)}, f32[16,4,512]{2,1,0:T(4,128)S(1)}, f32[3,256]{1,0:T(4,128)S(1)}, f32[16,64,512]{2,0,1:T(8,128)}, /*index=5*/s32[]{:T(128)}, s32[]{:T(128)}, s32[]{}) while((s32[]{:T(128)}, f32[16,256]{1,0:T(8,128)S(1)}, f32[16,4,512]{2,1,0:T(4,128)S(1)}, f32[3,256]{1,0:T(4,128)S(1)}, ...), condition=%wide.region_6.7_spmd.clone, body=%wide.region_2.6_spmd.clone.sunk | while | flops 31997980 | bytes 12545307 | solution.py:78
  151.3 19.5 %fusion.38 = (f32[8,256]{1,0:T(8,128)S(1)}, f32[8,256]{1,0:T(8,128)S(1)}) fusion(f32[8,512]{1,0:T(8,128)S(1)} %get-tuple-element.167, f32[256,512]{1,0:T(8,128)S(1)} %get-tuple-element.169, f32[8,512]{1,0:T(8,128)S(1)} %get-tuple-element.170, f32[8,512]{1,0:T(8,128)S(1)} %get-tuple-element.171, f32[8,512]{1,0:T(8,128)S(1)} %get-tuple-element.172, ...), kind=kLoop, calls=%fused_computation.8.clone.1 | loop fusion | flops 30404608 | bytes 3817504 | tf_op jit(solution)/shard_map/while/body/eval_jaxpr/reduce_sum | solution.py:58
  173.1 19.5 %fusion.38 = (f32[8,256]{1,0:T(8,128)S(1)}, f32[8,256]{1,0:T(8,128)S(1)}) fusion(f32[8,512]{1,0:T(8,128)S(1)} %get-tuple-element.167, f32[256,512]{1,0:T(8,128)S(1)} %get-tuple-element.169, f32[8,512]{1,0:T(8,128)S(1)} %get-tuple-element.170, f32[8,512]{1,0:T(8,128)S(1)} %get-tuple-element.171, f32[8,512]{1,0:T(8,128)S(1)} %get-tuple-element.172, ...), kind=kLoop, calls=%fused_computation.8.clone.1 | loop fusion | flops 30404608 | bytes 3817504 | tf_op jit(solution)/shard_map/while/body/eval_jaxpr/reduce_sum | solution.py:58
  194.8 19.5 %fusion.38 = (f32[8,256]{1,0:T(8,128)S(1)}, f32[8,256]{1,0:T(8,128)S(1)}) fusion(f32[8,512]{1,0:T(8,128)S(1)} %get-tuple-element.167, f32[256,512]{1,0:T(8,128)S(1)} %get-tuple-element.169, f32[8,512]{1,0:T(8,128)S(1)} %get-tuple-element.170, f32[8,512]{1,0:T(8,128)S(1)} %get-tuple-element.171, f32[8,512]{1,0:T(8,128)S(1)} %get-tuple-element.172, ...), kind=kLoop, calls=%fused_computation.8.clone.1 | loop fusion | flops 30404608 | bytes 3817504 | tf_op jit(solution)/shard_map/while/body/eval_jaxpr/reduce_sum | solution.py:58
  216.6 19.5 %fusion.38 = (f32[8,256]{1,0:T(8,128)S(1)}, f32[8,256]{1,0:T(8,128)S(1)}) fusion(f32[8,512]{1,0:T(8,128)S(1)} %get-tuple-element.167, f32[256,512]{1,0:T(8,128)S(1)} %get-tuple-element.169, f32[8,512]{1,0:T(8,128)S(1)} %get-tuple-element.170, f32[8,512]{1,0:T(8,128)S(1)} %get-tuple-element.171, f32[8,512]{1,0:T(8,128)S(1)} %get-tuple-element.172, ...), kind=kLoop, calls=%fused_computation.8.clone.1 | loop fusion | flops 30404608 | bytes 3817504 | tf_op jit(solution)/shard_map/while/body/eval_jaxpr/reduce_sum | solution.py:58
  238.3 19.5 %fusion.38 = (f32[8,256]{1,0:T(8,128)S(1)}, f32[8,256]{1,0:T(8,128)S(1)}) fusion(f32[8,512]{1,0:T(8,128)S(1)} %get-tuple-element.167, f32[256,512]{1,0:T(8,128)S(1)} %get-tuple-element.169, f32[8,512]{1,0:T(8,128)S(1)} %get-tuple-element.170, f32[8,512]{1,0:T(8,128)S(1)} %get-tuple-element.171, f32[8,512]{1,0:T(8,128)S(1)} %get-tuple-element.172, ...), kind=kLoop, calls=%fused_computation.8.clone.1 | loop fusion | flops 30404608 | bytes 3817504 | tf_op jit(solution)/shard_map/while/body/eval_jaxpr/reduce_sum | solution.py:58
  260.1 19.5 %fusion.38 = (f32[8,256]{1,0:T(8,128)S(1)}, f32[8,256]{1,0:T(8,128)S(1)}) fusion(f32[8,512]{1,0:T(8,128)S(1)} %get-tuple-element.167, f32[256,512]{1,0:T(8,128)S(1)} %get-tuple-element.169, f32[8,512]{1,0:T(8,128)S(1)} %get-tuple-element.170, f32[8,512]{1,0:T(8,128)S(1)} %get-tuple-element.171, f32[8,512]{1,0:T(8,128)S(1)} %get-tuple-element.172, ...), kind=kLoop, calls=%fused_computation.8.clone.1 | loop fusion | flops 30404608 | bytes 3817504 | tf_op jit(solution)/shard_map/while/body/eval_jaxpr/reduce_sum | solution.py:58
  281.8 19.5 %fusion.38 = (f32[8,256]{1,0:T(8,128)S(1)}, f32[8,256]{1,0:T(8,128)S(1)}) fusion(f32[8,512]{1,0:T(8,128)S(1)} %get-tuple-element.167, f32[256,512]{1,0:T(8,128)S(1)} %get-tuple-element.169, f32[8,512]{1,0:T(8,128)S(1)} %get-tuple-element.170, f32[8,512]{1,0:T(8,128)S(1)} %get-tuple-element.171, f32[8,512]{1,0:T(8,128)S(1)} %get-tuple-element.172, ...), kind=kLoop, calls=%fused_computation.8.clone.1 | loop fusion | flops 30404608 | bytes 3817504 | tf_op jit(solution)/shard_map/while/body/eval_jaxpr/reduce_sum | solution.py:58
  303.5 19.5 %fusion.38 = (f32[8,256]{1,0:T(8,128)S(1)}, f32[8,256]{1,0:T(8,128)S(1)}) fusion(f32[8,512]{1,0:T(8,128)S(1)} %get-tuple-element.167, f32[256,512]{1,0:T(8,128)S(1)} %get-tuple-element.169, f32[8,512]{1,0:T(8,128)S(1)} %get-tuple-element.170, f32[8,512]{1,0:T(8,128)S(1)} %get-tuple-element.171, f32[8,512]{1,0:T(8,128)S(1)} %get-tuple-element.172, ...), kind=kLoop, calls=%fused_computation.8.clone.1 | loop fusion | flops 30404608 | bytes 3817504 | tf_op jit(solution)/shard_map/while/body/eval_jaxpr/reduce_sum | solution.py:58
  325.3 19.5 %fusion.38 = (f32[8,256]{1,0:T(8,128)S(1)}, f32[8,256]{1,0:T(8,128)S(1)}) fusion(f32[8,512]{1,0:T(8,128)S(1)} %get-tuple-element.167, f32[256,512]{1,0:T(8,128)S(1)} %get-tuple-element.169, f32[8,512]{1,0:T(8,128)S(1)} %get-tuple-element.170, f32[8,512]{1,0:T(8,128)S(1)} %get-tuple-element.171, f32[8,512]{1,0:T(8,128)S(1)} %get-tuple-element.172, ...), kind=kLoop, calls=%fused_computation.8.clone.1 | loop fusion | flops 30404608 | bytes 3817504 | tf_op jit(solution)/shard_map/while/body/eval_jaxpr/reduce_sum | solution.py:58
  347.0 19.5 %fusion.38 = (f32[8,256]{1,0:T(8,128)S(1)}, f32[8,256]{1,0:T(8,128)S(1)}) fusion(f32[8,512]{1,0:T(8,128)S(1)} %get-tuple-element.167, f32[256,512]{1,0:T(8,128)S(1)} %get-tuple-element.169, f32[8,512]{1,0:T(8,128)S(1)} %get-tuple-element.170, f32[8,512]{1,0:T(8,128)S(1)} %get-tuple-element.171, f32[8,512]{1,0:T(8,128)S(1)} %get-tuple-element.172, ...), kind=kLoop, calls=%fused_computation.8.clone.1 | loop fusion | flops 30404608 | bytes 3817504 | tf_op jit(solution)/shard_map/while/body/eval_jaxpr/reduce_sum | solution.py:58
  368.8 19.5 %fusion.38 = (f32[8,256]{1,0:T(8,128)S(1)}, f32[8,256]{1,0:T(8,128)S(1)}) fusion(f32[8,512]{1,0:T(8,128)S(1)} %get-tuple-element.167, f32[256,512]{1,0:T(8,128)S(1)} %get-tuple-element.169, f32[8,512]{1,0:T(8,128)S(1)} %get-tuple-element.170, f32[8,512]{1,0:T(8,128)S(1)} %get-tuple-element.171, f32[8,512]{1,0:T(8,128)S(1)} %get-tuple-element.172, ...), kind=kLoop, calls=%fused_computation.8.clone.1 | loop fusion | flops 30404608 | bytes 3817504 | tf_op jit(solution)/shard_map/while/body/eval_jaxpr/reduce_sum | solution.py:58
  390.5 19.5 %fusion.38 = (f32[8,256]{1,0:T(8,128)S(1)}, f32[8,256]{1,0:T(8,128)S(1)}) fusion(f32[8,512]{1,0:T(8,128)S(1)} %get-tuple-element.167, f32[256,512]{1,0:T(8,128)S(1)} %get-tuple-element.169, f32[8,512]{1,0:T(8,128)S(1)} %get-tuple-element.170, f32[8,512]{1,0:T(8,128)S(1)} %get-tuple-element.171, f32[8,512]{1,0:T(8,128)S(1)} %get-tuple-element.172, ...), kind=kLoop, calls=%fused_computation.8.clone.1 | loop fusion | flops 30404608 | bytes 3817504 | tf_op jit(solution)/shard_map/while/body/eval_jaxpr/reduce_sum | solution.py:58
  412.3 19.5 %fusion.38 = (f32[8,256]{1,0:T(8,128)S(1)}, f32[8,256]{1,0:T(8,128)S(1)}) fusion(f32[8,512]{1,0:T(8,128)S(1)} %get-tuple-element.167, f32[256,512]{1,0:T(8,128)S(1)} %get-tuple-element.169, f32[8,512]{1,0:T(8,128)S(1)} %get-tuple-element.170, f32[8,512]{1,0:T(8,128)S(1)} %get-tuple-element.171, f32[8,512]{1,0:T(8,128)S(1)} %get-tuple-element.172, ...), kind=kLoop, calls=%fused_computation.8.clone.1 | loop fusion | flops 30404608 | bytes 3817504 | tf_op jit(solution)/shard_map/while/body/eval_jaxpr/reduce_sum | solution.py:58
  434.0 19.5 %fusion.38 = (f32[8,256]{1,0:T(8,128)S(1)}, f32[8,256]{1,0:T(8,128)S(1)}) fusion(f32[8,512]{1,0:T(8,128)S(1)} %get-tuple-element.167, f32[256,512]{1,0:T(8,128)S(1)} %get-tuple-element.169, f32[8,512]{1,0:T(8,128)S(1)} %get-tuple-element.170, f32[8,512]{1,0:T(8,128)S(1)} %get-tuple-element.171, f32[8,512]{1,0:T(8,128)S(1)} %get-tuple-element.172, ...), kind=kLoop, calls=%fused_computation.8.clone.1 | loop fusion | flops 30404608 | bytes 3817504 | tf_op jit(solution)/shard_map/while/body/eval_jaxpr/reduce_sum | solution.py:58
  455.8 19.5 %fusion.38 = (f32[8,256]{1,0:T(8,128)S(1)}, f32[8,256]{1,0:T(8,128)S(1)}) fusion(f32[8,512]{1,0:T(8,128)S(1)} %get-tuple-element.167, f32[256,512]{1,0:T(8,128)S(1)} %get-tuple-element.169, f32[8,512]{1,0:T(8,128)S(1)} %get-tuple-element.170, f32[8,512]{1,0:T(8,128)S(1)} %get-tuple-element.171, f32[8,512]{1,0:T(8,128)S(1)} %get-tuple-element.172, ...), kind=kLoop, calls=%fused_computation.8.clone.1 | loop fusion | flops 30404608 | bytes 3817504 | tf_op jit(solution)/shard_map/while/body/eval_jaxpr/reduce_sum | solution.py:58
  477.5 19.5 %fusion.38 = (f32[8,256]{1,0:T(8,128)S(1)}, f32[8,256]{1,0:T(8,128)S(1)}) fusion(f32[8,512]{1,0:T(8,128)S(1)} %get-tuple-element.167, f32[256,512]{1,0:T(8,128)S(1)} %get-tuple-element.169, f32[8,512]{1,0:T(8,128)S(1)} %get-tuple-element.170, f32[8,512]{1,0:T(8,128)S(1)} %get-tuple-element.171, f32[8,512]{1,0:T(8,128)S(1)} %get-tuple-element.172, ...), kind=kLoop, calls=%fused_computation.8.clone.1 | loop fusion | flops 30404608 | bytes 3817504 | tf_op jit(solution)/shard_map/while/body/eval_jaxpr/reduce_sum | solution.py:58
  497.1 26.4 %psum.7 = f32[16,256]{1,0:T(8,128)S(1)} all-reduce(f32[16,256]{1,0:T(8,128)S(1)} %get-tuple-element.32), channel_id=1, replica_groups=mesh['grp'=8,'obs'=16] {'grp'}, use_global_device_ids=true, to_apply=%region_7.8 | all-reduce | flops 4096 | bytes 32768 | tf_op jit(solution)/shard_map/psum | solution.py:125
  (201 shorter events, 47.7 us)
Async XLA Ops:
  8.7 16.3 %all-to-all-start.1 = ((s32[16,1,1]{2,1,0:T(1,128)}), s32[16,1,1]{2,1,0:T(1,128)S(1)}, u32[]{:S(2)}, u32[]{:S(2)}) async-start(s32[16,1,1]{2,1,0:T(1,128)} %copy.22), calls=%async_computation.1 | async-start | bytes 16384 | tf_op jit(solution)/shard_map/all_to_all | solution.py:102
  25.0 59.9 %all-to-all-start = ((bf16[16,4,256,128]{3,2,1,0:T(8,128)(2,1)}), bf16[16,4,256,128]{3,2,1,0:T(8,128)(2,1)}, u32[]{:S(2)}, u32[]{:S(2)}) async-start(bf16[16,4,256,128]{3,2,1,0:T(8,128)(2,1)} %copy.21), calls=%async_computation | async-start | bytes 8388608 | tf_op jit(solution)/shard_map/all_to_all | solution.py:101
  31.8 56.9 %copy-start.1 = (f32[4,512]{1,0:T(4,128)S(1)}, f32[4,512]{1,0:T(4,128)}, u32[]{:S(2)}) copy-start(f32[4,512]{1,0:T(4,128)} %param.10) | copy-start | bytes 24580
  31.9 113.1 %all-gather.2.cloned.1.call-start = ((), (), s32[]{:S(2)}) async-start(), calls=%async_computation.2 | async-start | bytes 2228224 | tf_op jit(solution)/shard_map/all_gather | solution.py:121
  85.0 64.2 %copy-start = (f32[3,256]{1,0:T(4,128)S(1)}, f32[3,256]{1,0:T(4,128)}, u32[]{:S(2)}) copy-start(f32[3,256]{1,0:T(4,128)} %param.11) | copy-start | bytes 9220
Sparse Core Ops, SparseCore 0:
  88.9 56.0 all-gather.1
where the time goes:
time: 538 us; the launch traced here: 531 us
  other arithmetic  324 us (60%)
  waiting for transfers between devices  79.9 us (15%)
  blocking collectives  55.6 us (10%)
  local copies, waits for them, and re-layouts  35.4 us (7%)
  starting transfers between devices  16.1 us (3%)
  between operations  14.1 us (3%)
    reduce_sum x16, other arithmetic, pressure_tiles(): press_re = jnp.sum(green_re * bracket_re - green_im * bracket_im, axis=2)  312 us
    all_to_all x1, waiting for transfers between devices, local(): lax.all_to_all(outgoing, 'obs', split_axis=0, concat_axis=0, tiled=True)  52.5 us
    all_gather x1, blocking collectives, local(): lax.all_gather(face_geom, 'obs', axis=1, tiled=True)  29.2 us
    all_gather x1, waiting for transfers between devices, local(): lax.all_gather(spec_wide, 'obs', axis=1, tiled=True)  27 us
    psum x1, blocking collectives, local(): summed = lax.psum(pressure, 'grp')  26.4 us
    dynamic_slice x32, local copies, waits for them, and re-layouts, accumulate(): result, _ = lax.scan(add_block, zero_sum, (spec_blocks, geom_blocks))  21.7 us
  transfers between devices with their start and end apart: 3, of which 3 were waited for; matrix products, arithmetic and copies ran while one was open for 1% of the time, Pallas kernels for 0%

commit v1 on v0

v1 whole, which is shorter than its diff:
```python
import math

import jax
import jax.numpy as jnp
import numpy as np
from jax import lax
from jax.experimental import pallas as pl
from jax.experimental.pallas import tpu as pltpu
from jax.sharding import PartitionSpec as P

SAMPLES = 256
NFREQ = 8
NSIG = 4
PATCH = 128
MAXP = 8
PER_OWN = 4
FACES_OWN = 512
CHANNELS = NSIG * 2 * NFREQ
ROWS_MSG = 96
OBS_ROW = 64
TAIL_ROW = 80
OBS_TILE = 256
CHUNK = 64
CHUNKS = FACES_OWN // CHUNK
TERMS = 32
CENTER_X = 15.0

COS_COEFS = (
    0.9999992107823207,
    -19.73898035576387,
    64.92865742102978,
    -85.27162153426406,
    58.790492119980826,
    -21.071105627415147,
)
SIN_COEFS = (
    6.283184916495429,
    -41.34158923268831,
    81.59994332977428,
    -76.61447253115396,
    41.342882354135696,
    -12.471243534350362,
)


def spectral_basis():
    t = np.arange(SAMPLES, dtype=np.float64)
    m = np.arange(1, NFREQ + 1, dtype=np.float64)
    angles = 2.0 * math.pi / SAMPLES * (t[:, None] * m[None, :])
    window = (0.5 - 0.5 * np.cos(2.0 * math.pi / SAMPLES * t)) * math.sqrt(8.0 / (3.0 * SAMPLES))
    table = np.concatenate(
        [window[:, None] * np.cos(angles), -window[:, None] * np.sin(angles)], axis=1
    )
    return jnp.asarray(table.T.astype(np.float32)).astype(jnp.bfloat16)


def pack_kernel(count_ref, place_ref, basis_ref, signals_ref, obs_ref, out_ref):
    sig = pl.program_id(0)

    @pl.when(sig == 0)
    def _():
        x = obs_ref[...]
        hi = x.astype(jnp.bfloat16).astype(jnp.float32)
        rest = x - hi
        mid = rest.astype(jnp.bfloat16).astype(jnp.float32)
        low = rest - mid
        rows = []
        for part in (hi, mid, low):
            for c in range(3):
                for h in range(2):
                    rows.append(part[c : c + 1, h * PATCH : (h + 1) * PATCH])
        head = jnp.concatenate(rows[:16], axis=0).astype(jnp.bfloat16)
        tail = jnp.concatenate(
            rows[16:] + [jnp.zeros((14, PATCH), jnp.float32)], axis=0
        )
        out_ref[...] = jnp.zeros_like(out_ref)
        for o in range(out_ref.shape[0]):
            out_ref[o, OBS_ROW:TAIL_ROW, :] = head
            out_ref[o, TAIL_ROW:, :] = tail.astype(jnp.bfloat16)
        row_id = lax.broadcasted_iota(jnp.int32, (16, PATCH), 0)
        for j in range(MAXP):
            place = place_ref[j]
            owner = place // PER_OWN
            part_no = (place % PER_OWN + 1).astype(jnp.float32)

            @pl.when(j < count_ref[0])
            def _():
                out_ref[owner, TAIL_ROW:, :] = jnp.where(row_id < 2, tail, part_no).astype(
                    jnp.bfloat16
                )

    spec = jnp.dot(
        basis_ref[...], signals_ref[0], preferred_element_type=jnp.float32
    ).astype(jnp.bfloat16)
    row0 = pl.multiple_of(sig * 16, 16)
    for j in range(MAXP):

        @pl.when(j < count_ref[0])
        def _():
            owner = place_ref[j] // PER_OWN
            out_ref[owner, pl.ds(row0, 16), :] = spec[:, j * PATCH : (j + 1) * PATCH]


def pack(signals, patch_count, patch_place, obs_pos, owners):
    return pl.pallas_call(
        pack_kernel,
        grid=(NSIG,),
        in_specs=[
            pl.BlockSpec(memory_space=pltpu.SMEM),
            pl.BlockSpec(memory_space=pltpu.SMEM),
            pl.BlockSpec((2 * NFREQ, SAMPLES), lambda s: (0, 0)),
            pl.BlockSpec((1, SAMPLES, MAXP * PATCH), lambda s: (s, 0, 0)),
            pl.BlockSpec(obs_pos.shape, lambda s: (0, 0)),
        ],
        out_specs=pl.BlockSpec((owners, ROWS_MSG, PATCH), lambda s: (0, 0, 0)),
        out_shape=jax.ShapeDtypeStruct((owners, ROWS_MSG, PATCH), jnp.bfloat16),
        name="pack",
    )(patch_count, patch_place, spectral_basis(), signals, obs_pos)


def horner(coefs, z):
    acc = jnp.full_like(z, coefs[-1])
    for c in coefs[-2::-1]:
        acc = acc * z + c
    return acc


def face_matrices(t, j, obs_ref, face_ref, g_ref):
    x = [obs_ref[t, c : c + 1, :] for c in range(3)]
    for group in range(CHUNK // 16):
        f0 = pl.multiple_of(j * CHUNK + group * 16, 16)
        cols = [face_ref[c, pl.ds(f0, 16), :] for c in range(4)]
        y = [jnp.concatenate([col, col], axis=1) for col in cols]
        dx = x[0] - y[0]
        dy = x[1] - y[1]
        dz = x[2] - y[2]
        r2 = dx * dx + dy * dy + dz * dz
        inv = lax.rsqrt(r2)
        r = r2 * inv
        turns = r * (0.25 / math.pi)
        frac = turns - jnp.floor(turns + 0.5)
        z = frac * frac
        cos1 = horner(COS_COEFS, z)
        sin1 = horner(SIN_COEFS, z) * frac
        amp = y[3] * inv * (inv * inv)
        two_cos = cos1 + cos1
        c_old, s_old = amp, None
        c_now, s_now = amp * cos1, amp * sin1
        for m in range(NFREQ):
            if m == 1:
                c_old, c_now = c_now, two_cos * c_now - c_old
                s_old, s_now = s_now, two_cos * s_now
            elif m > 1:
                c_old, c_now = c_now, two_cos * c_now - c_old
                s_old, s_now = s_now, two_cos * s_now - s_old
            g_ref[m, group * 16 : group * 16 + 16, :] = (c_now * r).astype(jnp.bfloat16)
            g_ref[m, CHUNK + group * 16 : CHUNK + group * 16 + 16, :] = (s_now * r).astype(
                jnp.bfloat16
            )
            g_ref[m, 2 * CHUNK + group * 16 : 2 * CHUNK + group * 16 + 16, :] = c_now.astype(
                jnp.bfloat16
            )
            g_ref[m, 3 * CHUNK + group * 16 : 3 * CHUNK + group * 16 + 16, :] = s_now.astype(
                jnp.bfloat16
            )


def face_products(j, w_ref, g_ref, acc_ref):
    first = j == 0
    for m in range(NFREQ):
        part = jnp.dot(w_ref[j, m], g_ref[m], preferred_element_type=jnp.float32)
        acc_ref[m] = jnp.where(first, 0.0, acc_ref[m]) + part


def finish_tile(t, obs_ref, acc_ref, out_ref):
    x = [obs_ref[t, c : c + 1, :] for c in range(3)]
    xx = x[0] * x[0] + x[1] * x[1] + x[2] * x[2]
    for m in range(NFREQ):
        k = 0.5 * (m + 1)
        for part in range(2):
            row = lambda n: acc_ref[m, 2 * n + part : 2 * n + part + 1, :]
            total = row(0) + row(1) + xx * row(2)
            for c in range(3):
                total = total + x[c] * (row(3 + c) + row(6 + c))
            at = part * NFREQ + m
            out_ref[t, at : at + 1, :] = total * (k / (4.0 * math.pi))


def pressure_kernel(w_ref, geom_ref, obs_ref, out_ref, face_ref, ga_ref, gb_ref, acc_ref):
    tiles = obs_ref.shape[0]
    geom = jnp.concatenate([geom_ref[...], jnp.zeros((4, FACES_OWN), jnp.float32)], axis=0)
    cols = geom.T
    for c in range(4):
        face_ref[c] = jnp.broadcast_to(cols[:, c : c + 1], (FACES_OWN, PATCH))

    def pair(t, jj):
        face_matrices(t, 2 * jj, obs_ref, face_ref, ga_ref)
        return None

    def step(i, carry):
        t = i // (CHUNKS // 2)
        jj = i % (CHUNKS // 2)
        t_old = jnp.where(jj == 0, t - 1, t)
        j_old = jnp.where(jj == 0, CHUNKS - 1, 2 * jj - 1)
        face_matrices(t, 2 * jj, obs_ref, face_ref, ga_ref)
        face_products(j_old, w_ref, gb_ref, acc_ref)

        @pl.when(jnp.logical_and(jj == 0, t > 0))
        def _():
            finish_tile(t_old, obs_ref, acc_ref, out_ref)

        face_matrices(t, 2 * jj + 1, obs_ref, face_ref, gb_ref)
        face_products(2 * jj, w_ref, ga_ref, acc_ref)
        return carry

    lax.fori_loop(0, tiles * (CHUNKS // 2), step, 0)
    face_products(CHUNKS - 1, w_ref, gb_ref, acc_ref)
    finish_tile(tiles - 1, obs_ref, acc_ref, out_ref)


def partial_pressure(weights, geom, observers):
    tiles = observers.shape[0]
    return pl.pallas_call(
        pressure_kernel,
        in_specs=[pl.BlockSpec(memory_space=pltpu.VMEM)] * 3,
        out_specs=pl.BlockSpec(memory_space=pltpu.VMEM),
        out_shape=jax.ShapeDtypeStruct((tiles, 2 * NFREQ, OBS_TILE), jnp.float32),
        scratch_shapes=[
            pltpu.VMEM((4, FACES_OWN, PATCH), jnp.float32),
            pltpu.VMEM((NFREQ, 4 * CHUNK, OBS_TILE), jnp.bfloat16),
            pltpu.VMEM((NFREQ, 4 * CHUNK, OBS_TILE), jnp.bfloat16),
            pltpu.VMEM((NFREQ, TERMS, OBS_TILE), jnp.float32),
        ],
        compiler_params=pltpu.CompilerParams(vmem_limit_bytes=48 * 1024 * 1024),
        name="pressure",
    )(weights, geom, observers)


def face_weights(spec, geom):
    k = (0.5 * jnp.arange(1, NFREQ + 1, dtype=jnp.float32))[:, None]
    y = geom[:3]
    yy = jnp.sum(y * y, axis=0)[None]
    qr, qi = spec[0, 0], spec[0, 1]
    lr = [spec[1 + c, 0] for c in range(3)]
    li = [spec[1 + c, 1] for c in range(3)]
    lyr = sum(lr[c] * y[c][None] for c in range(3))
    lyi = sum(li[c] * y[c][None] for c in range(3))
    zero = jnp.zeros_like(qr)

    def four(load_r, load_i, mono):
        re = (-load_i, load_r, load_r / k - mono * qi, load_i / k + mono * qr)
        im = (load_r, load_i, load_i / k + mono * qr, -load_r / k + mono * qi)
        return [jnp.stack(re), jnp.stack(im)]

    def split(v):
        hi = lax.reduce_precision(v, 8, 7)
        return hi, v - hi

    base = [split(v) for v in four(-lyr, -lyi, yy)]
    load = [[split(v) for v in four(lr[c], li[c], -2.0 * y[c][None])] for c in range(3)]
    square = four(zero, zero, jnp.ones_like(yy))
    rows = [base[p][0] for p in range(2)] + [base[p][1] for p in range(2)] + square
    rows += [load[c][p][0] for c in range(3) for p in range(2)]
    rows += [load[c][p][1] for c in range(3) for p in range(2)]
    rows += [jnp.zeros_like(rows[0])] * (TERMS - len(rows))
    w = jnp.stack(rows)
    w = w.reshape(TERMS, 4, NFREQ, CHUNKS, CHUNK).transpose(3, 2, 0, 1, 4)
    return w.reshape(CHUNKS, NFREQ, TERMS, 4 * CHUNK).astype(jnp.bfloat16)


def local(signals, patch_count, patch_place, face_geom, obs_pos):
    owners = lax.axis_size("obs")
    groups = lax.axis_size("grp")
    outgoing = pack(signals, patch_count, patch_place, obs_pos, owners)
    arrived = lax.all_to_all(outgoing, "obs", split_axis=0, concat_axis=0, tiled=True)
    header = arrived[:, ROWS_MSG - 1, 0]
    owned = (header[:, None] == jnp.arange(1, PER_OWN + 1).astype(jnp.bfloat16)[None, :]).astype(
        jnp.bfloat16
    )
    spec = jnp.einsum(
        "oj,okp->kjp", owned, arrived[:, :CHANNELS], preferred_element_type=jnp.float32
    ).reshape(NSIG, 2, NFREQ, FACES_OWN)
    parts = arrived[:, OBS_ROW : OBS_ROW + 18].astype(jnp.float32)
    parts = parts.reshape(owners, 3, 3, OBS_TILE)
    observers = (parts[:, 0] + parts[:, 1]) + parts[:, 2]
    shift = jnp.asarray([CENTER_X, 0.0, 0.0], jnp.float32)
    observers = observers - shift[None, :, None]
    geom = face_geom - jnp.asarray([CENTER_X, 0.0, 0.0, 0.0], jnp.float32)[:, None]
    out = partial_pressure(face_weights(spec, geom), geom, observers)
    out = out.reshape(owners * groups, 2 * NFREQ // groups, OBS_TILE)
    got = lax.all_to_all(out, ("obs", "grp"), split_axis=0, concat_axis=0, tiled=True)
    return jnp.sum(got, axis=0)


def solution(mesh):
    return jax.shard_map(
        local,
        mesh=mesh,
        in_specs=(
            P(None, None, ("grp", "obs")),
            P(("grp", "obs")),
            P(("grp", "obs")),
            P(None, ("grp", "obs")),
            P(None, "obs"),
        ),
        out_specs=P("grp", "obs"),
        check_vma=False,
    )
```

time: 538 us -> 87.6 us (0.16); the launches traced: 531 us -> 87.3 us
  other arithmetic: 324 us -> 3.02 us
  waiting for transfers between devices: 79.9 us -> 8.72 us
  Pallas kernels: 0 us -> 42.9 us
  blocking collectives: 55.6 us -> 16.6 us
  local copies, waits for them, and re-layouts: 35.4 us -> 5.43 us
  between operations: 14.1 us -> 1.03 us
  starting transfers between devices: 16.1 us -> 9.33 us
    reduce_sum x17 -> x2, other arithmetic: 312 us -> 0.74 us  [the longest x1 0.72 us: local(): return jnp.sum(got, axis=0)]
    all_to_all x1, waiting for transfers between devices: 52.5 us -> 8.72 us  [local(): lax.all_to_all(outgoing, 'obs', split_axis=0, concat_axis=0, tiled=True)]
    pallas_call x0 -> x2, Pallas kernels: none -> 42.9 us  [the longest x1 39.2 us: partial_pressure(): pl.pallas_call(pressure_kernel, in_specs=[pl.BlockSpec(memory_space=pltpu...]
    all_gather x1 -> x0, blocking collectives: 29.2 us -> none  [local(): lax.all_gather(face_geom, 'obs', axis=1, tiled=True)]
    all_gather x1 -> x0, waiting for transfers between devices: 27 us -> none  [local(): lax.all_gather(spec_wide, 'obs', axis=1, tiled=True)]
    psum x1 -> x0, blocking collectives: 26.4 us -> none  [local(): summed = lax.psum(pressure, 'grp')]
    dynamic_slice x33 -> x0, local copies, waits for them, and re-layouts: 22.3 us -> none  [the longest x32 21.7 us: accumulate(): result, _ = lax.scan(add_block, zero_sum, (spec_blocks, geom_blocks))]
    all_to_all x0 -> x1, blocking collectives: none -> 16.6 us  [local(): lax.all_to_all(out, ('obs', 'grp'), split_axis=0, concat_axis=0, tiled=True)]
  transfers between devices with their start and end apart: 3 -> 1, of which waited for: 3 -> 1; matrix products, arithmetic and copies ran while one was open for 1% -> 2% of each run, Pallas kernels for 0% -> 0%
where the time goes in v1:
time: 87.6 us; the launch traced here: 87.3 us
  Pallas kernels  42.9 us (49%)
  blocking collectives  16.6 us (19%)
  starting transfers between devices  9.33 us (11%)
  waiting for transfers between devices  8.72 us (10%)
  local copies, waits for them, and re-layouts  5.43 us (6%)
  other arithmetic  3.02 us (3%)
  between operations  1.03 us (1%)
    pallas_call x1, Pallas kernels, partial_pressure(): pl.pallas_call(pressure_kernel, in_specs=[pl.BlockSpec(memory_space=pltpu...  39.2 us
    all_to_all x1, blocking collectives, local(): lax.all_to_all(out, ('obs', 'grp'), split_axis=0, concat_axis=0, tiled=True)  16.6 us
    all_to_all x1, starting transfers between devices, local(): lax.all_to_all(outgoing, 'obs', split_axis=0, concat_axis=0, tiled=True)  9.33 us
    all_to_all x1, waiting for transfers between devices, local(): lax.all_to_all(outgoing, 'obs', split_axis=0, concat_axis=0, tiled=True)  8.72 us
    pallas_call x1, Pallas kernels, pack(): pl.pallas_call(pack_kernel, grid=(NSIG,), in_specs=[pl.BlockSpec(memory_s...  3.64 us
  transfers between devices with their start and end apart: 1, of which 1 were waited for; matrix products, arithmetic and copies ran while one was open for 2% of the time, Pallas kernels for 0%

profile of v1, /device:TPU:1, one launch (start us, length us, event | category | flops | bytes accessed | tf_op | source)
XLA Modules:
  0.0 87.3 jit_solution(1627190441249072473)
XLA Ops:
  0.7 3.6 %pack.1 = bf16[16,96,128]{2,1,0:T(8,128)(2,1)} custom-call(s32[1]{0:T(128)S(6)} %copy.91.count_ref, s32[8]{0:T(128)} %place_ref.1, bf16[16,256]{1,0:T(8,128)(2,1)} %constant.34.basis_ref, bf16[4,256,1024]{2,1,0:T(8,128)(2,1)} %signals_ref.1, f32[3,256]{1,0:T(4,128)} %obs_ref.1), custom_call_target="tpu_custom_call" | custom-call | tf_op jit(solution)/shard_map/pack/pallas_call | solution.py:105
  4.3 9.3 %all-to-all-start = ((bf16[16,96,128]{2,1,0:T(8,128)(2,1)}), bf16[16,96,128]{2,1,0:T(8,128)(2,1)S(1)}, u32[]{:S(2)}, u32[]{:S(2)}) async-start(bf16[16,96,128]{2,1,0:T(8,128)(2,1)} %pack.1), calls=%async_computation | async-start | bytes 786432 | tf_op jit(solution)/shard_map/all_to_all | solution.py:275
  14.4 0.6 broadcast_divide_fusion
  15.0 8.7 %all-to-all-done = bf16[16,96,128]{2,1,0:T(8,128)(2,1)S(1)} async-done(((bf16[16,96,128]{2,1,0:T(8,128)(2,1)}), bf16[16,96,128]{2,1,0:T(8,128)(2,1)S(1)}, u32[]{:S(2)}, u32[]{:S(2)}) %all-to-all-start) | async-done | bytes 393248 | tf_op jit(solution)/shard_map/all_to_all | solution.py:275
  23.8 0.2 slice_reduce_fusion
  24.0 0.3 convolution_bitcast_fusion
  25.6 0.1 add_bitcast_fusion.1
  25.7 0.1 negate_bitcast_fusion.4
  25.9 0.8 add_convert_fusion
  26.8 0.1 copy_dynamic-update-slice_fusion.14
  27.1 0.1 copy_dynamic-update-slice_fusion.12
  27.1 0.2 maximum_dynamic-update-slice_fusion
  27.4 0.1 copy_dynamic-update-slice_fusion.10
  28.1 0.1 copy_dynamic-update-slice_fusion.4
  28.3 0.1 copy_dynamic-update-slice_fusion.2
  28.4 0.1 copy_dynamic-update-slice_fusion
  28.6 0.1 broadcast_dynamic-update-slice_fusion.1
  28.7 0.2 broadcast_dynamic-update-slice_fusion
  28.9 1.4 %convert_element_type.20.w_ref = bf16[8,8,32,256]{3,2,1,0:T(8,128)(2,1)S(1)} reshape(bf16[8,8,32,4,64]{4,3,2,1,0:T(4,128)(2,1)S(1)} %bitcast.97) | data formatting | bytes 2097152 | tf_op jit(solution)/shard_map/convert_element_type | solution.py:268
  30.4 0.1 reshape.2981
  30.6 39.2 %pressure.1 = f32[16,16,256]{2,1,0:T(8,128)S(1)} custom-call(bf16[8,8,32,256]{3,2,1,0:T(8,128)(2,1)S(1)} %convert_element_type.20.w_ref, f32[4,512]{1,0:T(4,128)S(1)} %broadcast_add_fusion.geom_ref, f32[16,3,256]{2,1,0:T(4,128)S(1)} %fusion.11.obs_ref), custom_call_target="tpu_custom_call" | custom-call | tf_op jit(solution)/shard_map/pressure/pallas_call | solution.py:223
  69.8 0.1 reshape.2979
  70.0 16.6 %all_to_all.10 = f32[128,2,256]{2,1,0:T(2,128)S(1)} all-to-all(f32[128,2,256]{2,1,0:T(2,128)S(1)} %reshape.2979), channel_id=1, replica_groups=mesh['grp'=8,'obs'=16] {'obs','grp'}, dimensions={0} | all-to-all | bytes 524288 | tf_op jit(solution)/shard_map/all_to_all | solution.py:291
  86.5 0.7 reduce_sum.19
  (63 shorter events, 3.4 us)
Async XLA Ops:
  0.0 13.7 %copy-start.3 = (f32[4]{0:T(128)S(1)}, f32[4]{0:T(128)}, u32[]{:S(2)}) copy-start(f32[4]{0:T(128)} %constant.35) | copy-start | bytes 52
  0.0 13.7 %copy-start = (f32[4,512]{1,0:T(4,128)S(1)}, f32[4,512]{1,0:T(4,128)}, u32[]{:S(2)}) copy-start(f32[4,512]{1,0:T(4,128)} %param.11) | copy-start | bytes 24580
  4.3 19.4 %all-to-all-start = ((bf16[16,96,128]{2,1,0:T(8,128)(2,1)}), bf16[16,96,128]{2,1,0:T(8,128)(2,1)S(1)}, u32[]{:S(2)}, u32[]{:S(2)}) async-start(bf16[16,96,128]{2,1,0:T(8,128)(2,1)} %pack.1), calls=%async_computation | async-start | bytes 786432 | tf_op jit(solution)/shard_map/all_to_all | solution.py:275
  24.3 1.6 %copy-start.2 = (f32[8]{0:T(128)S(1)}, f32[8]{0:T(128)}, u32[]{:S(2)}) copy-start(f32[8]{0:T(128)} %get-tuple-element.81) | copy-start | bytes 100
  28.7 1.8 %copy-start.1 = (f32[3]{0:T(128)S(1)}, f32[3]{0:T(128)}, u32[]{:S(2)}) copy-start(f32[3]{0:T(128)} %constant.36) | copy-start | bytes 40

commit v2 on v1

v2 whole, which is shorter than its diff:
```python
import math

import jax
import jax.numpy as jnp
import numpy as np
from jax import lax
from jax.experimental import pallas as pl
from jax.experimental.pallas import tpu as pltpu
from jax.sharding import PartitionSpec as P

SAMPLES = 256
NFREQ = 8
NSIG = 4
PATCH = 128
MAXP = 8
PER_OWN = 4
FACES_OWN = 512
CHANNELS = NSIG * 2 * NFREQ
ROWS_MSG = 80
OBS_ROW = 64
OBS_TILE = 256
CHUNK = 64
TERMS = 16
HALF = FACES_OWN // 2
HALF_CHUNKS = HALF // CHUNK
UNIT = 0.25 / math.pi
CENTER_X = 15.0

COS_COEFS = (
    0.9999992107823207,
    -19.73898035576387,
    64.92865742102978,
    -85.27162153426406,
    58.790492119980826,
    -21.071105627415147,
)
SIN_COEFS = (
    6.283184916495429,
    -41.34158923268831,
    81.59994332977428,
    -76.61447253115396,
    41.342882354135696,
    -12.471243534350362,
)


def spectral_basis():
    t = np.arange(SAMPLES, dtype=np.float64)
    m = np.arange(1, NFREQ + 1, dtype=np.float64)
    angles = 2.0 * math.pi / SAMPLES * (t[:, None] * m[None, :])
    window = (0.5 - 0.5 * np.cos(2.0 * math.pi / SAMPLES * t)) * math.sqrt(8.0 / (3.0 * SAMPLES))
    table = np.concatenate(
        [window[:, None] * np.cos(angles), -window[:, None] * np.sin(angles)], axis=1
    )
    return jnp.asarray(table.T.astype(np.float32)).astype(jnp.bfloat16)


def pack_kernel(count_ref, place_ref, basis_ref, signals_ref, obs_ref, out_ref):
    sig = pl.program_id(0)

    @pl.when(sig == 0)
    def _():
        x = obs_ref[...]
        hi = x.astype(jnp.bfloat16).astype(jnp.float32)
        rows = []
        for part in (hi, x - hi):
            for c in range(3):
                for h in range(2):
                    rows.append(part[c : c + 1, h * PATCH : (h + 1) * PATCH])
        tail = jnp.concatenate(rows + [jnp.zeros((4, PATCH), jnp.float32)], axis=0)
        out_ref[...] = jnp.zeros_like(out_ref)
        for o in range(out_ref.shape[0]):
            out_ref[o, OBS_ROW:, :] = tail.astype(jnp.bfloat16)
        row_id = lax.broadcasted_iota(jnp.int32, (16, PATCH), 0)
        for j in range(MAXP):
            place = place_ref[j]
            owner = place // PER_OWN
            part_no = (place % PER_OWN + 1).astype(jnp.float32)

            @pl.when(j < count_ref[0])
            def _():
                out_ref[owner, OBS_ROW:, :] = jnp.where(row_id < 12, tail, part_no).astype(
                    jnp.bfloat16
                )

    spec = jnp.dot(
        basis_ref[...], signals_ref[0], preferred_element_type=jnp.float32
    ).astype(jnp.bfloat16)
    row0 = pl.multiple_of(sig * 16, 16)
    for j in range(MAXP):

        @pl.when(j < count_ref[0])
        def _():
            owner = place_ref[j] // PER_OWN
            out_ref[owner, pl.ds(row0, 16), :] = spec[:, j * PATCH : (j + 1) * PATCH]


def pack(signals, patch_count, patch_place, obs_pos, owners):
    return pl.pallas_call(
        pack_kernel,
        grid=(NSIG,),
        in_specs=[
            pl.BlockSpec(memory_space=pltpu.SMEM),
            pl.BlockSpec(memory_space=pltpu.SMEM),
            pl.BlockSpec((2 * NFREQ, SAMPLES), lambda s: (0, 0)),
            pl.BlockSpec((1, SAMPLES, MAXP * PATCH), lambda s: (s, 0, 0)),
            pl.BlockSpec(obs_pos.shape, lambda s: (0, 0)),
        ],
        out_specs=pl.BlockSpec((owners, ROWS_MSG, PATCH), lambda s: (0, 0, 0)),
        out_shape=jax.ShapeDtypeStruct((owners, ROWS_MSG, PATCH), jnp.bfloat16),
        name="pack",
    )(patch_count, patch_place, spectral_basis(), signals, obs_pos)


def horner(coefs, z):
    acc = jnp.full_like(z, coefs[-1])
    for c in coefs[-2::-1]:
        acc = acc * z + c
    return acc


def face_matrices(t, f0, at, obs_ref, face_ref, g_ref):
    x = [obs_ref[t, c : c + 1, :] for c in range(3)]
    for group in range(CHUNK // 16):
        y = []
        for c in range(4):
            col = face_ref[c, f0 + group * 16 : f0 + group * 16 + 16, :]
            y.append(jnp.concatenate([col, col], axis=1))
        dx = x[0] - y[0]
        dy = x[1] - y[1]
        dz = x[2] - y[2]
        r2 = dx * dx + dy * dy + dz * dz
        inv = lax.rsqrt(r2)
        r = r2 * inv
        frac = r - jnp.round(r)
        z = frac * frac
        cos1 = horner(COS_COEFS, z)
        sin1 = horner(SIN_COEFS, z) * frac
        amp = y[3] * inv * (inv * inv)
        two_cos = cos1 + cos1
        c_old, s_old = amp, None
        c_now, s_now = amp * cos1, amp * sin1
        for m in range(NFREQ):
            if m == 1:
                c_old, c_now = c_now, two_cos * c_now - c_old
                s_old, s_now = s_now, two_cos * s_now
            elif m > 1:
                c_old, c_now = c_now, two_cos * c_now - c_old
                s_old, s_now = s_now, two_cos * s_now - s_old
            for family, v in enumerate((c_now * r, s_now * r, c_now, s_now)):
                row = family * HALF + at + group * 16
                g_ref[m, row : row + 16, :] = v.astype(jnp.bfloat16)


def half_product(m, half, w_ref, g_ref):
    return jnp.dot(
        w_ref[m, :, half * 4 * HALF : (half + 1) * 4 * HALF],
        g_ref[m],
        preferred_element_type=jnp.float32,
    )


def finish(t, m, total, obs_ref, out_ref):
    x = [obs_ref[t, c : c + 1, :] for c in range(3)]
    xx = x[0] * x[0] + x[1] * x[1] + x[2] * x[2]
    scale = 0.5 * (m + 1) / (16.0 * math.pi**2)
    for part in range(2):
        row = lambda n: total[2 * n + part : 2 * n + part + 1, :]
        value = xx * row(0) + row(1) + row(2)
        value = value + x[0] * (row(3) + row(6)) + x[1] * (row(4) + row(7)) + x[2] * row(5)
        value = value * scale
        at = part * NFREQ + m
        for h in range(2):
            line = 2 * (at % 2) + h
            out_ref[at // 2, t, line : line + 1, :] = value[:, h * PATCH : (h + 1) * PATCH]


def build_observers(arrived_ref, obs_ref):
    for t in range(arrived_ref.shape[0]):
        rows = arrived_ref[t, OBS_ROW : OBS_ROW + 16, :].astype(jnp.float32)
        pos = rows[0:6] + rows[6:12]
        for c in range(3):
            line = jnp.concatenate([pos[2 * c : 2 * c + 1], pos[2 * c + 1 : 2 * c + 2]], axis=1)
            line = (line - CENTER_X if c == 0 else line) * UNIT
            obs_ref[t, c : c + 1, :] = line


def build_faces(geom_ref, geo_ref, face_ref):
    geo_ref[0:1, :] = (geom_ref[0:1, :] - CENTER_X) * UNIT
    geo_ref[1:3, :] = geom_ref[1:3, :] * UNIT
    geo_ref[3:4, :] = geom_ref[3:4, :]
    geo_ref[4:8, :] = jnp.zeros((4, FACES_OWN), jnp.float32)
    cols = geo_ref[...].T
    for c in range(4):
        face_ref[c] = jnp.broadcast_to(cols[:, c : c + 1], (FACES_OWN, PATCH))


def build_weights(arrived_ref, geo_ref, wide_ref, w_ref):
    inv_k = 1.0 / (
        2.0
        * math.pi
        * (1 + lax.broadcasted_iota(jnp.int32, (NFREQ, PATCH), 0)).astype(jnp.float32)
    )
    for j in range(PER_OWN):
        spec = jnp.zeros((CHANNELS, PATCH), jnp.float32)
        for o in range(arrived_ref.shape[0]):
            tail = arrived_ref[o, OBS_ROW : OBS_ROW + 16, :].astype(jnp.float32)
            picked = (tail[15:16, :] == float(j + 1)).astype(jnp.float32)
            spec = spec + arrived_ref[o, 0:CHANNELS, :].astype(jnp.float32) * picked
        y = [geo_ref[c : c + 1, j * PATCH : (j + 1) * PATCH] for c in range(3)]
        yy = y[0] * y[0] + y[1] * y[1] + y[2] * y[2]
        qr, qi = spec[0:8], spec[8:16]
        lr = [spec[16 + 16 * c : 24 + 16 * c] for c in range(3)]
        li = [spec[24 + 16 * c : 32 + 16 * c] for c in range(3)]
        lyr = lr[0] * y[0] + lr[1] * y[1] + lr[2] * y[2]
        lyi = li[0] * y[0] + li[1] * y[1] + li[2] * y[2]
        zero = jnp.zeros_like(qr)

        def four(load_r, load_i, mono):
            near_r, near_i = load_r * inv_k, load_i * inv_k
            mono_r, mono_i = mono * qr, mono * qi
            return (
                (-load_i, load_r, near_r - mono_i, near_i + mono_r),
                (load_r, load_i, near_i + mono_r, mono_i - near_r),
            )

        half, at = divmod(j * PATCH, HALF)

        def put(term, family, value):
            block = ((half * 4 + family) * HALF + at) // PATCH
            wide_ref[block, pl.ds(term, NFREQ, stride=TERMS), :] = value

        square = ((zero, zero, -qi, qr), (zero, zero, qr, qi))
        base = four(-lyr, -lyi, yy)
        load = [four(lr[c], li[c], -2.0 * y[c]) for c in range(3)]
        for part in range(2):
            for family in range(4):
                put(part, family, square[part][family])
                hi = base[part][family].astype(jnp.bfloat16).astype(jnp.float32)
                put(2 + part, family, hi)
                put(4 + part, family, base[part][family] - hi)
                for c in range(3):
                    value = load[c][part][family]
                    hi = value.astype(jnp.bfloat16).astype(jnp.float32)
                    put(6 + 2 * c + part, family, hi)
                    if c < 2:
                        put(12 + 2 * c + part, family, value - hi)
    for m in range(NFREQ):
        for block in range(wide_ref.shape[0]):
            w_ref[m, :, block * PATCH : (block + 1) * PATCH] = wide_ref[
                block, m * TERMS : (m + 1) * TERMS, :
            ].astype(jnp.bfloat16)


def pressure_kernel(
    arrived_ref, geom_ref, out_ref, obs_ref, geo_ref, face_ref, wide_ref, w_ref, ga_ref, gb_ref, acc_ref
):
    tiles = arrived_ref.shape[0]
    build_observers(arrived_ref, obs_ref)
    build_faces(geom_ref, geo_ref, face_ref)
    build_weights(arrived_ref, geo_ref, wide_ref, w_ref)
    per_chunk = NFREQ // HALF_CHUNKS

    def tile(t, carry):
        before = jnp.maximum(t - 1, 0)
        for j in range(HALF_CHUNKS):
            face_matrices(t, j * CHUNK, j * CHUNK, obs_ref, face_ref, ga_ref)
            for m in range(j * per_chunk, (j + 1) * per_chunk):
                total = acc_ref[m] + half_product(m, 1, w_ref, gb_ref)
                finish(before, m, total, obs_ref, out_ref)
        for j in range(HALF_CHUNKS):
            face_matrices(t, HALF + j * CHUNK, j * CHUNK, obs_ref, face_ref, gb_ref)
            for m in range(j * per_chunk, (j + 1) * per_chunk):
                acc_ref[m] = half_product(m, 0, w_ref, ga_ref)
        return carry

    lax.fori_loop(0, tiles, tile, 0)
    for m in range(NFREQ):
        total = acc_ref[m] + half_product(m, 1, w_ref, gb_ref)
        finish(tiles - 1, m, total, obs_ref, out_ref)


def partial_pressure(arrived, geom):
    tiles = arrived.shape[0]
    return pl.pallas_call(
        pressure_kernel,
        in_specs=[pl.BlockSpec(memory_space=pltpu.VMEM)] * 2,
        out_specs=pl.BlockSpec(memory_space=pltpu.VMEM),
        out_shape=jax.ShapeDtypeStruct((NFREQ, tiles, 4, PATCH), jnp.float32),
        scratch_shapes=[
            pltpu.VMEM((tiles, 8, OBS_TILE), jnp.float32),
            pltpu.VMEM((8, FACES_OWN), jnp.float32),
            pltpu.VMEM((4, FACES_OWN, PATCH), jnp.float32),
            pltpu.VMEM((4 * FACES_OWN // PATCH, NFREQ * TERMS, PATCH), jnp.float32),
            pltpu.VMEM((NFREQ, TERMS, 4 * FACES_OWN), jnp.bfloat16),
            pltpu.VMEM((NFREQ, 4 * HALF, OBS_TILE), jnp.bfloat16),
            pltpu.VMEM((NFREQ, 4 * HALF, OBS_TILE), jnp.bfloat16),
            pltpu.VMEM((NFREQ, TERMS, OBS_TILE), jnp.float32),
        ],
        compiler_params=pltpu.CompilerParams(vmem_limit_bytes=48 * 1024 * 1024),
        name="pressure",
    )(arrived, geom)


def local(signals, patch_count, patch_place, face_geom, obs_pos):
    owners = lax.axis_size("obs")
    groups = lax.axis_size("grp")
    outgoing = pack(signals, patch_count, patch_place, obs_pos, owners)
    arrived = lax.all_to_all(outgoing, "obs", split_axis=0, concat_axis=0, tiled=True)
    out = partial_pressure(arrived, face_geom)
    out = out.reshape(groups * owners, 4, PATCH)
    got = lax.all_to_all(out, ("grp", "obs"), split_axis=0, concat_axis=0, tiled=True)
    return jnp.sum(got, axis=0).reshape(2 * NFREQ // groups, OBS_TILE)


def solution(mesh):
    return jax.shard_map(
        local,
        mesh=mesh,
        in_specs=(
            P(None, None, ("grp", "obs")),
            P(("grp", "obs")),
            P(("grp", "obs")),
            P(None, ("grp", "obs")),
            P(None, "obs"),
        ),
        out_specs=P("grp", "obs"),
        check_vma=False,
    )
```

time: 87.6 us -> 82.7 us (0.944)
  blocking collectives: 16.6 us -> 35 us
  starting transfers between devices: 9.33 us -> 0 us
  waiting for transfers between devices: 8.72 us -> 0 us
  local copies, waits for them, and re-layouts: 5.43 us -> 0.6 us
  Pallas kernels: 42.9 us -> 46 us
  other arithmetic: 3.02 us -> 0.14 us
    all_to_all x1 -> x2, blocking collectives: 16.6 us -> 35 us  [the longest x1 18.8 us: local(): lax.all_to_all(outgoing, 'obs', split_axis=0, concat_axis=0, tiled=True)]
    all_to_all x1 -> x0, starting transfers between devices: 9.33 us -> none  [local(): lax.all_to_all(outgoing, 'obs', split_axis=0, concat_axis=0, tiled=True)]
    all_to_all x1 -> x0, waiting for transfers between devices: 8.72 us -> none  [local(): lax.all_to_all(outgoing, 'obs', split_axis=0, concat_axis=0, tiled=True)]
    pallas_call x1, Pallas kernels: 39.2 us -> 42.4 us  [partial_pressure(): pl.pallas_call(pressure_kernel, in_specs=[pl.BlockSpec(memory_space=pltpu...]
    unnamed x27 -> x2, local copies, waits for them, and re-layouts: 1.51 us -> 0.01 us
    convert_element_type x1 -> x0, local copies, waits for them, and re-layouts: 1.4 us -> none  [face_weights(): return w.reshape(CHUNKS, NFREQ, TERMS, 4 * CHUNK).astype(jnp.bfloat16)]
    another operation x9 -> x0, other arithmetic: 1.3 us -> none
  transfers between devices with their start and end apart: 1 -> 0, of which waited for: 1 -> 0; matrix products, arithmetic and copies ran while one was open for 2% -> 0% of each run, Pallas kernels for 0% -> 0%
where the time goes in v2:
time: 82.7 us; the launch traced here: 82.4 us
  Pallas kernels  46 us (56%)
  blocking collectives  35 us (42%)
    pallas_call x1, Pallas kernels, partial_pressure(): pl.pallas_call(pressure_kernel, in_specs=[pl.BlockSpec(memory_space=pltpu...  42.4 us
    all_to_all x1, blocking collectives, local(): lax.all_to_all(outgoing, 'obs', split_axis=0, concat_axis=0, tiled=True)  18.8 us
    all_to_all x1, blocking collectives, local(): lax.all_to_all(out, ('grp', 'obs'), split_axis=0, concat_axis=0, tiled=True)  16.2 us
    pallas_call x1, Pallas kernels, pack(): pl.pallas_call(pack_kernel, grid=(NSIG,), in_specs=[pl.BlockSpec(memory_s...  3.57 us

profile of v2, /device:TPU:1, one launch (start us, length us, event | category | flops | bytes accessed | tf_op | source)
XLA Modules:
  0.0 82.4 jit_solution(5553634824856369491)
XLA Ops:
  0.0 0.0 copy-start
  0.7 3.6 %pack.1 = bf16[16,80,128]{2,1,0:T(8,128)(2,1)} custom-call(s32[1]{0:T(128)S(6)} %copy.7.count_ref, s32[8]{0:T(128)} %place_ref.1, bf16[16,256]{1,0:T(8,128)(2,1)} %constant.7.basis_ref, bf16[4,256,1024]{2,1,0:T(8,128)(2,1)} %signals_ref.1, f32[3,256]{1,0:T(4,128)} %obs_ref.1), custom_call_target="tpu_custom_call" | custom-call | tf_op jit(solution)/shard_map/pack/pallas_call | solution.py:99
  4.2 18.8 %all_to_all.10.arrived_ref = bf16[16,80,128]{2,1,0:T(8,128)(2,1)S(1)} all-to-all(bf16[16,80,128]{2,1,0:T(8,128)(2,1)} %pack.1), channel_id=1, replica_groups=mesh['grp'=8,'obs'=16] {'obs'}, dimensions={0} | all-to-all | bytes 655360 | tf_op jit(solution)/shard_map/all_to_all | solution.py:309
  23.0 0.0 copy-done
  23.0 42.4 %pressure.1 = f32[8,16,4,128]{3,2,1,0:T(4,128)S(1)} custom-call(bf16[16,80,128]{2,1,0:T(8,128)(2,1)S(1)} %all_to_all.10.arrived_ref, f32[4,512]{1,0:T(4,128)S(1)} %copy-done), custom_call_target="tpu_custom_call" | custom-call | tf_op jit(solution)/shard_map/pressure/pallas_call | solution.py:285
  65.4 16.2 %all_to_all.11 = f32[128,4,128]{2,1,0:T(4,128)S(1)} all-to-all(f32[128,4,128]{2,1,0:T(4,128)S(1)} %bitcast.1), channel_id=1, replica_groups=mesh['grp'=8,'obs'=16] {'grp','obs'}, dimensions={0} | all-to-all | bytes 524288 | tf_op jit(solution)/shard_map/all_to_all | solution.py:312
  81.6 0.1 reduce_sum.9
  81.8 0.6 reshape.7
Async XLA Ops:
  0.0 23.0 %copy-start = (f32[4,512]{1,0:T(4,128)S(1)}, f32[4,512]{1,0:T(4,128)}, u32[]{:S(2)}) copy-start(f32[4,512]{1,0:T(4,128)} %geom_ref.1) | copy-start | bytes 24580

commit v3 on v2

--- a/solution.py
+++ b/solution.py
@@ -19,10 +19,9 @@
 ROWS_MSG = 80
 OBS_ROW = 64
 OBS_TILE = 256
+TERMS = 16
 CHUNK = 64
-TERMS = 16
-HALF = FACES_OWN // 2
-HALF_CHUNKS = HALF // CHUNK
+CHUNKS = FACES_OWN // CHUNK
 UNIT = 0.25 / math.pi
 CENTER_X = 15.0
 
@@ -119,60 +118,57 @@
     return acc
 
 
-def face_matrices(t, f0, at, obs_ref, face_ref, g_ref):
-    x = [obs_ref[t, c : c + 1, :] for c in range(3)]
+def add_chunk(t, chunk, obs_ref, face_ref, w_ref, acc_ref):
+    state = []
+    x = [obs_ref[t, c : c + 1, :] for c in range(4)]
     for group in range(CHUNK // 16):
+        rows = slice(chunk * CHUNK + group * 16, chunk * CHUNK + group * 16 + 16)
         y = []
-        for c in range(4):
-            col = face_ref[c, f0 + group * 16 : f0 + group * 16 + 16, :]
+        for c in range(5):
+            col = face_ref[c, rows, :]
             y.append(jnp.concatenate([col, col], axis=1))
-        dx = x[0] - y[0]
-        dy = x[1] - y[1]
-        dz = x[2] - y[2]
-        r2 = dx * dx + dy * dy + dz * dz
+        r2 = (x[3] + y[3]) + x[0] * y[0] + x[1] * y[1] + x[2] * y[2]
         inv = lax.rsqrt(r2)
         r = r2 * inv
+        amp = y[4] * (inv * inv)
         frac = r - jnp.round(r)
         z = frac * frac
         cos1 = horner(COS_COEFS, z)
         sin1 = horner(SIN_COEFS, z) * frac
-        amp = y[3] * inv * (inv * inv)
-        two_cos = cos1 + cos1
-        c_old, s_old = amp, None
-        c_now, s_now = amp * cos1, amp * sin1
-        for m in range(NFREQ):
+        state.append([cos1 + cos1, inv.astype(jnp.bfloat16), amp, amp * cos1, None, amp * sin1])
+    for m in range(NFREQ):
+        pieces = []
+        for one in state:
+            two_cos, other, c_old, c_now, s_old, s_now = one
             if m == 1:
                 c_old, c_now = c_now, two_cos * c_now - c_old
                 s_old, s_now = s_now, two_cos * s_now
             elif m > 1:
                 c_old, c_now = c_now, two_cos * c_now - c_old
                 s_old, s_now = s_now, two_cos * s_now - s_old
-            for family, v in enumerate((c_now * r, s_now * r, c_now, s_now)):
-                row = family * HALF + at + group * 16
-                g_ref[m, row : row + 16, :] = v.astype(jnp.bfloat16)
-
-
-def half_product(m, half, w_ref, g_ref):
-    return jnp.dot(
-        w_ref[m, :, half * 4 * HALF : (half + 1) * 4 * HALF],
-        g_ref[m],
-        preferred_element_type=jnp.float32,
-    )
-
-
-def finish(t, m, total, obs_ref, out_ref):
+            one[2:] = [c_old, c_now, s_old, s_now]
+            c_half, s_half = c_now.astype(jnp.bfloat16), s_now.astype(jnp.bfloat16)
+            pieces.append((c_half, s_half, c_half * other, s_half * other))
+        g = jnp.concatenate([p[family] for family in range(4) for p in pieces], axis=0)
+        part = jnp.dot(w_ref[chunk, m], g, preferred_element_type=jnp.float32)
+        acc_ref[m] = part if chunk == 0 else acc_ref[m] + part
+
+
+def finish(t, obs_ref, acc_ref, out_ref):
     x = [obs_ref[t, c : c + 1, :] for c in range(3)]
-    xx = x[0] * x[0] + x[1] * x[1] + x[2] * x[2]
-    scale = 0.5 * (m + 1) / (16.0 * math.pi**2)
-    for part in range(2):
-        row = lambda n: total[2 * n + part : 2 * n + part + 1, :]
-        value = xx * row(0) + row(1) + row(2)
-        value = value + x[0] * (row(3) + row(6)) + x[1] * (row(4) + row(7)) + x[2] * row(5)
-        value = value * scale
-        at = part * NFREQ + m
-        for h in range(2):
-            line = 2 * (at % 2) + h
-            out_ref[at // 2, t, line : line + 1, :] = value[:, h * PATCH : (h + 1) * PATCH]
+    xx = obs_ref[t, 3:4, :]
+    for m in range(NFREQ):
+        total = acc_ref[m]
+        scale = 0.5 * (m + 1) / (16.0 * math.pi**2)
+        for part in range(2):
+            row = lambda n: total[2 * n + part : 2 * n + part + 1, :]
+            value = xx * row(0) + row(1) + row(2)
+            value = value + x[0] * (row(3) + row(6)) + x[1] * (row(4) + row(7)) + x[2] * row(5)
+            value = value * scale
+            at = part * NFREQ + m
+            for h in range(2):
+                line = 2 * (at % 2) + h
+                out_ref[at // 2, t, line : line + 1, :] = value[:, h * PATCH : (h + 1) * PATCH]
 
 
 def build_observers(arrived_ref, obs_ref):
@@ -183,16 +179,21 @@
             line = jnp.concatenate([pos[2 * c : 2 * c + 1], pos[2 * c + 1 : 2 * c + 2]], axis=1)
             line = (line - CENTER_X if c == 0 else line) * UNIT
             obs_ref[t, c : c + 1, :] = line
+        x = [obs_ref[t, c : c + 1, :] for c in range(3)]
+        obs_ref[t, 3:4, :] = x[0] * x[0] + x[1] * x[1] + x[2] * x[2]
 
 
 def build_faces(geom_ref, geo_ref, face_ref):
     geo_ref[0:1, :] = (geom_ref[0:1, :] - CENTER_X) * UNIT
     geo_ref[1:3, :] = geom_ref[1:3, :] * UNIT
-    geo_ref[3:4, :] = geom_ref[3:4, :]
-    geo_ref[4:8, :] = jnp.zeros((4, FACES_OWN), jnp.float32)
+    y = [geo_ref[c : c + 1, :] for c in range(3)]
+    for c in range(3):
+        geo_ref[4 + c : 5 + c, :] = -2.0 * y[c]
+    geo_ref[3:4, :] = y[0] * y[0] + y[1] * y[1] + y[2] * y[2]
+    geo_ref[7:8, :] = geom_ref[3:4, :]
     cols = geo_ref[...].T
-    for c in range(4):
-        face_ref[c] = jnp.broadcast_to(cols[:, c : c + 1], (FACES_OWN, PATCH))
+    for c, row in enumerate((4, 5, 6, 3, 7)):
+        face_ref[c] = jnp.broadcast_to(cols[:, row : row + 1], (FACES_OWN, PATCH))
 
 
 def build_weights(arrived_ref, geo_ref, wide_ref, w_ref):
@@ -201,6 +202,7 @@
         * math.pi
         * (1 + lax.broadcasted_iota(jnp.int32, (NFREQ, PATCH), 0)).astype(jnp.float32)
     )
+    left = lax.broadcasted_iota(jnp.int32, (NFREQ, PATCH), 1) < CHUNK
     for j in range(PER_OWN):
         spec = jnp.zeros((CHANNELS, PATCH), jnp.float32)
         for o in range(arrived_ref.shape[0]):
@@ -208,7 +210,7 @@
             picked = (tail[15:16, :] == float(j + 1)).astype(jnp.float32)
             spec = spec + arrived_ref[o, 0:CHANNELS, :].astype(jnp.float32) * picked
         y = [geo_ref[c : c + 1, j * PATCH : (j + 1) * PATCH] for c in range(3)]
-        yy = y[0] * y[0] + y[1] * y[1] + y[2] * y[2]
+        yy = geo_ref[3:4, j * PATCH : (j + 1) * PATCH]
         qr, qi = spec[0:8], spec[8:16]
         lr = [spec[16 + 16 * c : 24 + 16 * c] for c in range(3)]
         li = [spec[24 + 16 * c : 32 + 16 * c] for c in range(3)]
@@ -224,60 +226,59 @@
                 (load_r, load_i, near_i + mono_r, mono_i - near_r),
             )
 
-        half, at = divmod(j * PATCH, HALF)
-
-        def put(term, family, value):
-            block = ((half * 4 + family) * HALF + at) // PATCH
-            wide_ref[block, pl.ds(term, NFREQ, stride=TERMS), :] = value
+        def put(term, values):
+            for pair in range(2):
+                a, b = values[2 * pair], values[2 * pair + 1]
+                first = jnp.where(left, a, pltpu.roll(b, CHUNK, axis=1))
+                second = jnp.where(left, pltpu.roll(a, CHUNK, axis=1), b)
+                rows = pl.ds(term, NFREQ, stride=TERMS)
+                wide_ref[4 * j + pair, rows, :] = first
+                wide_ref[4 * j + 2 + pair, rows, :] = second
 
         square = ((zero, zero, -qi, qr), (zero, zero, qr, qi))
         base = four(-lyr, -lyi, yy)
         load = [four(lr[c], li[c], -2.0 * y[c]) for c in range(3)]
+        def split(values):
+            hi = [v.astype(jnp.bfloat16).astype(jnp.float32) for v in values]
+            return hi, [v - h for v, h in zip(values, hi)]
+
         for part in range(2):
-            for family in range(4):
-                put(part, family, square[part][family])
-                hi = base[part][family].astype(jnp.bfloat16).astype(jnp.float32)
-                put(2 + part, family, hi)
-                put(4 + part, family, base[part][family] - hi)
-                for c in range(3):
-                    value = load[c][part][family]
-                    hi = value.astype(jnp.bfloat16).astype(jnp.float32)
-                    put(6 + 2 * c + part, family, hi)
-                    if c < 2:
-                        put(12 + 2 * c + part, family, value - hi)
-    for m in range(NFREQ):
-        for block in range(wide_ref.shape[0]):
-            w_ref[m, :, block * PATCH : (block + 1) * PATCH] = wide_ref[
-                block, m * TERMS : (m + 1) * TERMS, :
-            ].astype(jnp.bfloat16)
+            put(part, square[part])
+            hi, low = split(base[part])
+            put(2 + part, hi)
+            put(4 + part, low)
+            for c in range(3):
+                hi, low = split(load[c][part])
+                put(6 + 2 * c + part, hi)
+                if c < 2:
+                    put(12 + 2 * c + part, low)
+    for chunk in range(CHUNKS):
+        for m in range(NFREQ):
+            for side in range(2):
+                w_ref[chunk, m, :, side * PATCH : (side + 1) * PATCH] = wide_ref[
+                    2 * chunk + side, m * TERMS : (m + 1) * TERMS, :
+                ].astype(jnp.bfloat16)
 
 
 def pressure_kernel(
-    arrived_ref, geom_ref, out_ref, obs_ref, geo_ref, face_ref, wide_ref, w_ref, ga_ref, gb_ref, acc_ref
+    arrived_ref, geom_ref, out_ref, obs_ref, geo_ref, face_ref, wide_ref, w_ref, acc_ref
 ):
     tiles = arrived_ref.shape[0]
     build_observers(arrived_ref, obs_ref)
     build_faces(geom_ref, geo_ref, face_ref)
     build_weights(arrived_ref, geo_ref, wide_ref, w_ref)
-    per_chunk = NFREQ // HALF_CHUNKS
 
     def tile(t, carry):
-        before = jnp.maximum(t - 1, 0)
-        for j in range(HALF_CHUNKS):
-            face_matrices(t, j * CHUNK, j * CHUNK, obs_ref, face_ref, ga_ref)
-            for m in range(j * per_chunk, (j + 1) * per_chunk):
-                total = acc_ref[m] + half_product(m, 1, w_ref, gb_ref)
-                finish(before, m, total, obs_ref, out_ref)
-        for j in range(HALF_CHUNKS):
-            face_matrices(t, HALF + j * CHUNK, j * CHUNK, obs_ref, face_ref, gb_ref)
-            for m in range(j * per_chunk, (j + 1) * per_chunk):
-                acc_ref[m] = half_product(m, 0, w_ref, ga_ref)
+        finish(jnp.maximum(t - 1, 0), obs_ref, acc_ref, out_ref)
+        for chunk in range(CHUNKS):
+            add_chunk(t, chunk, obs_ref, face_ref, w_ref, acc_ref)
         return carry
 
-    lax.fori_loop(0, tiles, tile, 0)
-    for m in range(NFREQ):
-        total = acc_ref[m] + half_product(m, 1, w_ref, gb_ref)
-        finish(tiles - 1, m, total, obs_ref, out_ref)
+    def pair(i, carry):
+        return tile(2 * i + 1, tile(2 * i, carry))
+
+    lax.fori_loop(0, tiles // 2, pair, 0)
+    finish(tiles - 1, obs_ref, acc_ref, out_ref)
 
 
 def partial_pressure(arrived, geom):
@@ -290,11 +291,9 @@
         scratch_shapes=[
             pltpu.VMEM((tiles, 8, OBS_TILE), jnp.float32),
             pltpu.VMEM((8, FACES_OWN), jnp.float32),
-            pltpu.VMEM((4, FACES_OWN, PATCH), jnp.float32),
+            pltpu.VMEM((5, FACES_OWN, PATCH), jnp.float32),
             pltpu.VMEM((4 * FACES_OWN // PATCH, NFREQ * TERMS, PATCH), jnp.float32),
-            pltpu.VMEM((NFREQ, TERMS, 4 * FACES_OWN), jnp.bfloat16),
-            pltpu.VMEM((NFREQ, 4 * HALF, OBS_TILE), jnp.bfloat16),
-            pltpu.VMEM((NFREQ, 4 * HALF, OBS_TILE), jnp.bfloat16),
+            pltpu.VMEM((CHUNKS, NFREQ, TERMS, 4 * CHUNK), jnp.bfloat16),
             pltpu.VMEM((NFREQ, TERMS, OBS_TILE), jnp.float32),
         ],
         compiler_params=pltpu.CompilerParams(vmem_limit_bytes=48 * 1024 * 1024),

time: 82.7 us -> 69.3 us (0.84)
  Pallas kernels: 46 us -> 32.6 us
    pallas_call x1, Pallas kernels: 42.4 us -> 29 us  [partial_pressure(): pl.pallas_call(pressure_kernel, in_specs=[pl.BlockSpec(memory_space=pltpu...]
where the time goes in v3:
time: 69.3 us; the launch traced here: 69 us
  blocking collectives  35 us (51%)
  Pallas kernels  32.6 us (47%)
    pallas_call x1, Pallas kernels, partial_pressure(): pl.pallas_call(pressure_kernel, in_specs=[pl.BlockSpec(memory_space=pltpu...  29 us
    all_to_all x1, blocking collectives, local(): lax.all_to_all(outgoing, 'obs', split_axis=0, concat_axis=0, tiled=True)  18.8 us
    all_to_all x1, blocking collectives, local(): lax.all_to_all(out, ('grp', 'obs'), split_axis=0, concat_axis=0, tiled=True)  16.2 us
    pallas_call x1, Pallas kernels, pack(): pl.pallas_call(pack_kernel, grid=(NSIG,), in_specs=[pl.BlockSpec(memory_s...  3.59 us

profile of v3, /device:TPU:1, one launch (start us, length us, event | category | flops | bytes accessed | tf_op | source)
XLA Modules:
  0.0 69.0 jit_solution(8732465130388259971)
XLA Ops:
  0.0 0.0 copy-start
  0.7 3.6 %pack.1 = bf16[16,80,128]{2,1,0:T(8,128)(2,1)} custom-call(s32[1]{0:T(128)S(6)} %copy.7.count_ref, s32[8]{0:T(128)} %place_ref.1, bf16[16,256]{1,0:T(8,128)(2,1)} %constant.7.basis_ref, bf16[4,256,1024]{2,1,0:T(8,128)(2,1)} %signals_ref.1, f32[3,256]{1,0:T(4,128)} %obs_ref.1), custom_call_target="tpu_custom_call" | custom-call | tf_op jit(solution)/shard_map/pack/pallas_call | solution.py:98
  4.3 18.8 %all_to_all.10.arrived_ref = bf16[16,80,128]{2,1,0:T(8,128)(2,1)S(1)} all-to-all(bf16[16,80,128]{2,1,0:T(8,128)(2,1)} %pack.1), channel_id=1, replica_groups=mesh['grp'=8,'obs'=16] {'obs'}, dimensions={0} | all-to-all | bytes 655360 | tf_op jit(solution)/shard_map/all_to_all | solution.py:308
  23.0 0.0 copy-done
  23.0 29.0 %pressure.1 = f32[8,16,4,128]{3,2,1,0:T(4,128)S(1)} custom-call(bf16[16,80,128]{2,1,0:T(8,128)(2,1)S(1)} %all_to_all.10.arrived_ref, f32[4,512]{1,0:T(4,128)S(1)} %copy-done), custom_call_target="tpu_custom_call" | custom-call | tf_op jit(solution)/shard_map/pressure/pallas_call | solution.py:286
  52.1 16.2 %all_to_all.11 = f32[128,4,128]{2,1,0:T(4,128)S(1)} all-to-all(f32[128,4,128]{2,1,0:T(4,128)S(1)} %bitcast.1), channel_id=1, replica_groups=mesh['grp'=8,'obs'=16] {'grp','obs'}, dimensions={0} | all-to-all | bytes 524288 | tf_op jit(solution)/shard_map/all_to_all | solution.py:311
  68.3 0.1 reduce_sum.9
  68.4 0.6 reshape.7
Async XLA Ops:
  0.0 23.0 %copy-start = (f32[4,512]{1,0:T(4,128)S(1)}, f32[4,512]{1,0:T(4,128)}, u32[]{:S(2)}) copy-start(f32[4,512]{1,0:T(4,128)} %geom_ref.1) | copy-start | bytes 24580

commit v4 on v3

--- a/solution.py
+++ b/solution.py
@@ -54,61 +54,73 @@
     return jnp.asarray(table.T.astype(np.float32)).astype(jnp.bfloat16)
 
 
-def pack_kernel(count_ref, place_ref, basis_ref, signals_ref, obs_ref, out_ref):
-    sig = pl.program_id(0)
-
-    @pl.when(sig == 0)
-    def _():
-        x = obs_ref[...]
-        hi = x.astype(jnp.bfloat16).astype(jnp.float32)
-        rows = []
-        for part in (hi, x - hi):
-            for c in range(3):
-                for h in range(2):
-                    rows.append(part[c : c + 1, h * PATCH : (h + 1) * PATCH])
-        tail = jnp.concatenate(rows + [jnp.zeros((4, PATCH), jnp.float32)], axis=0)
-        out_ref[...] = jnp.zeros_like(out_ref)
-        for o in range(out_ref.shape[0]):
-            out_ref[o, OBS_ROW:, :] = tail.astype(jnp.bfloat16)
-        row_id = lax.broadcasted_iota(jnp.int32, (16, PATCH), 0)
+def pack_kernel(
+    count_hbm, place_hbm, basis_ref, signals_hbm, obs_ref, out_ref, count_ref, place_ref, rows_ref, sems
+):
+    small = [
+        pltpu.make_async_copy(count_hbm, count_ref, sems.at[NSIG]),
+        pltpu.make_async_copy(place_hbm, place_ref, sems.at[NSIG + 1]),
+    ]
+    large = [
+        pltpu.make_async_copy(signals_hbm.at[s], rows_ref.at[s], sems.at[s]) for s in range(NSIG)
+    ]
+    for copy in small + large:
+        copy.start()
+    x = obs_ref[...]
+    hi = x.astype(jnp.bfloat16).astype(jnp.float32)
+    rows = []
+    for part in (hi, x - hi):
+        for c in range(3):
+            for h in range(2):
+                rows.append(part[c : c + 1, h * PATCH : (h + 1) * PATCH])
+    tail = jnp.concatenate(rows + [jnp.zeros((4, PATCH), jnp.float32)], axis=0)
+    for o in range(out_ref.shape[0]):
+        out_ref[o, 0:CHANNELS, :] = jnp.zeros((CHANNELS, PATCH), jnp.bfloat16)
+        out_ref[o, OBS_ROW:, :] = tail.astype(jnp.bfloat16)
+    row_id = lax.broadcasted_iota(jnp.int32, (16, PATCH), 0)
+    for copy in small:
+        copy.wait()
+    count = count_ref[0, 0]
+    for j in range(MAXP):
+        place = place_ref[j]
+        part_no = (place % PER_OWN + 1).astype(jnp.float32)
+
+        @pl.when(j < count)
+        def _():
+            out_ref[place // PER_OWN, OBS_ROW:, :] = jnp.where(row_id < 12, tail, part_no).astype(
+                jnp.bfloat16
+            )
+
+    for s in range(NSIG):
+        large[s].wait()
+        spec = jnp.dot(
+            basis_ref[...], rows_ref[s], preferred_element_type=jnp.float32
+        ).astype(jnp.bfloat16)
         for j in range(MAXP):
-            place = place_ref[j]
-            owner = place // PER_OWN
-            part_no = (place % PER_OWN + 1).astype(jnp.float32)
-
-            @pl.when(j < count_ref[0])
+
+            @pl.when(j < count)
             def _():
-                out_ref[owner, OBS_ROW:, :] = jnp.where(row_id < 12, tail, part_no).astype(
-                    jnp.bfloat16
-                )
-
-    spec = jnp.dot(
-        basis_ref[...], signals_ref[0], preferred_element_type=jnp.float32
-    ).astype(jnp.bfloat16)
-    row0 = pl.multiple_of(sig * 16, 16)
-    for j in range(MAXP):
-
-        @pl.when(j < count_ref[0])
-        def _():
-            owner = place_ref[j] // PER_OWN
-            out_ref[owner, pl.ds(row0, 16), :] = spec[:, j * PATCH : (j + 1) * PATCH]
+                owner = place_ref[j] // PER_OWN
+                out_ref[owner, s * 16 : s * 16 + 16, :] = spec[:, j * PATCH : (j + 1) * PATCH]
 
 
 def pack(signals, patch_count, patch_place, obs_pos, owners):
+    hbm = pl.BlockSpec(memory_space=pltpu.MemorySpace.HBM)
+    vmem = pl.BlockSpec(memory_space=pltpu.VMEM)
     return pl.pallas_call(
         pack_kernel,
-        grid=(NSIG,),
-        in_specs=[
-            pl.BlockSpec(memory_space=pltpu.SMEM),
-            pl.BlockSpec(memory_space=pltpu.SMEM),
-            pl.BlockSpec((2 * NFREQ, SAMPLES), lambda s: (0, 0)),
-            pl.BlockSpec((1, SAMPLES, MAXP * PATCH), lambda s: (s, 0, 0)),
-            pl.BlockSpec(obs_pos.shape, lambda s: (0, 0)),
+        in_specs=[hbm, hbm, vmem, hbm, vmem],
+        out_specs=vmem,
+        out_shape=jax.ShapeDtypeStruct((owners, ROWS_MSG, PATCH), jnp.bfloat16),
+        scratch_shapes=[
+            pltpu.SMEM((1, 1), jnp.int32),
+            pltpu.SMEM((MAXP,), jnp.int32),
+            pltpu.VMEM(signals.shape, signals.dtype),
+            pltpu.SemaphoreType.DMA((NSIG + 2,)),
         ],
-        out_specs=pl.BlockSpec((owners, ROWS_MSG, PATCH), lambda s: (0, 0, 0)),
-        out_shape=jax.ShapeDtypeStruct((owners, ROWS_MSG, PATCH), jnp.bfloat16),
+        compiler_params=pltpu.CompilerParams(vmem_limit_bytes=67000000),
         name="pack",
-    )(patch_count, patch_place, spectral_basis(), signals, obs_pos)
+    )(patch_count.reshape(1, 1), patch_place, spectral_basis(), signals, obs_pos)
 
 
 def horner(coefs, z):
@@ -157,18 +169,20 @@
 def finish(t, obs_ref, acc_ref, out_ref):
     x = [obs_ref[t, c : c + 1, :] for c in range(3)]
     xx = obs_ref[t, 3:4, :]
-    for m in range(NFREQ):
-        total = acc_ref[m]
-        scale = 0.5 * (m + 1) / (16.0 * math.pi**2)
+    for pair in range(NFREQ // 2):
+        lines = ([], [])
+        for m in (2 * pair, 2 * pair + 1):
+            total = acc_ref[m]
+            scale = 0.5 * (m + 1) / (16.0 * math.pi**2)
+            for part in range(2):
+                row = lambda n: total[2 * n + part : 2 * n + part + 1, :]
+                value = xx * row(0) + row(1) + row(2)
+                value = value + x[0] * (row(3) + row(6)) + x[1] * (row(4) + row(7)) + x[2] * row(5)
+                value = value * scale
+                lines[part].extend([value[:, 0:PATCH], value[:, PATCH:]])
         for part in range(2):
-            row = lambda n: total[2 * n + part : 2 * n + part + 1, :]
-            value = xx * row(0) + row(1) + row(2)
-            value = value + x[0] * (row(3) + row(6)) + x[1] * (row(4) + row(7)) + x[2] * row(5)
-            value = value * scale
-            at = part * NFREQ + m
-            for h in range(2):
-                line = 2 * (at % 2) + h
-                out_ref[at // 2, t, line : line + 1, :] = value[:, h * PATCH : (h + 1) * PATCH]
+            block = jnp.concatenate(lines[part], axis=0)
+            out_ref[part * (NFREQ // 2) + pair, t] = block.astype(out_ref.dtype)
 
 
 def build_observers(arrived_ref, obs_ref):
@@ -287,7 +301,7 @@
         pressure_kernel,
         in_specs=[pl.BlockSpec(memory_space=pltpu.VMEM)] * 2,
         out_specs=pl.BlockSpec(memory_space=pltpu.VMEM),
-        out_shape=jax.ShapeDtypeStruct((NFREQ, tiles, 4, PATCH), jnp.float32),
+        out_shape=jax.ShapeDtypeStruct((NFREQ, tiles, 4, PATCH), jnp.bfloat16),
         scratch_shapes=[
             pltpu.VMEM((tiles, 8, OBS_TILE), jnp.float32),
             pltpu.VMEM((8, FACES_OWN), jnp.float32),
@@ -309,7 +323,7 @@
     out = partial_pressure(arrived, face_geom)
     out = out.reshape(groups * owners, 4, PATCH)
     got = lax.all_to_all(out, ("grp", "obs"), split_axis=0, concat_axis=0, tiled=True)
-    return jnp.sum(got, axis=0).reshape(2 * NFREQ // groups, OBS_TILE)
+    return jnp.sum(got.astype(jnp.float32), axis=0).reshape(2 * NFREQ // groups, OBS_TILE)
 
 
 def solution(mesh):

time: 69.3 us -> 68.1 us (0.983)
  blocking collectives: 35 us -> 34.1 us
    all_to_all x1, blocking collectives: 16.2 us -> 15.3 us  [local(): lax.all_to_all(out, ('grp', 'obs'), split_axis=0, concat_axis=0, tiled=True)]
where the time goes in v4:
time: 68.1 us; the launch traced here: 67.8 us
  blocking collectives  34.1 us (50%)
  Pallas kernels  32.3 us (47%)
    pallas_call x1, Pallas kernels, partial_pressure(): pl.pallas_call(pressure_kernel, in_specs=[pl.BlockSpec(memory_space=pltpu...  29.1 us
    all_to_all x1, blocking collectives, local(): lax.all_to_all(outgoing, 'obs', split_axis=0, concat_axis=0, tiled=True)  18.8 us
    all_to_all x1, blocking collectives, local(): lax.all_to_all(out, ('grp', 'obs'), split_axis=0, concat_axis=0, tiled=True)  15.3 us
    pallas_call x1, Pallas kernels, pack(): pl.pallas_call(pack_kernel, in_specs=[hbm, hbm, vmem, hbm, vmem], out_spe...  3.26 us

profile of v4, /device:TPU:1, one launch (start us, length us, event | category | flops | bytes accessed | tf_op | source)
XLA Modules:
  0.0 67.8 jit_solution(14515642913258137173)
XLA Ops:
  0.0 0.0 copy-start
  0.7 3.3 %pack.1 = bf16[16,80,128]{2,1,0:T(8,128)(2,1)} custom-call(s32[1,1]{1,0:T(1,128)} %bitcast.2.count_hbm, s32[8]{0:T(128)} %place_hbm.1, bf16[16,256]{1,0:T(8,128)(2,1)} %constant.7.basis_ref, bf16[4,256,1024]{2,1,0:T(8,128)(2,1)} %signals_hbm.1, f32[3,256]{1,0:T(4,128)} %obs_ref.1), custom_call_target="tpu_custom_call" | custom-call | tf_op jit(solution)/shard_map/pack/pallas_call | solution.py:110
  3.9 18.8 %all_to_all.10.arrived_ref = bf16[16,80,128]{2,1,0:T(8,128)(2,1)S(1)} all-to-all(bf16[16,80,128]{2,1,0:T(8,128)(2,1)} %pack.1), channel_id=1, replica_groups=mesh['grp'=8,'obs'=16] {'obs'}, dimensions={0} | all-to-all | bytes 655360 | tf_op jit(solution)/shard_map/all_to_all | solution.py:322
  22.7 0.0 copy-done
  22.7 29.1 %pressure.1 = bf16[8,16,4,128]{3,2,1,0:T(4,128)(2,1)S(1)} custom-call(bf16[16,80,128]{2,1,0:T(8,128)(2,1)S(1)} %all_to_all.10.arrived_ref, f32[4,512]{1,0:T(4,128)S(1)} %copy-done), custom_call_target="tpu_custom_call" | custom-call | tf_op jit(solution)/shard_map/pressure/pallas_call | solution.py:300
  51.8 15.3 %all_to_all.11 = bf16[128,4,128]{2,1,0:T(4,128)(2,1)S(1)} all-to-all(bf16[128,4,128]{2,1,0:T(4,128)(2,1)S(1)} %bitcast.3), channel_id=1, replica_groups=mesh['grp'=8,'obs'=16] {'grp','obs'}, dimensions={0} | all-to-all | bytes 262144 | tf_op jit(solution)/shard_map/all_to_all | solution.py:325
  67.1 0.1 convert_reduce_fusion
  67.2 0.6 reshape.11
Async XLA Ops:
  0.0 22.7 %copy-start = (f32[4,512]{1,0:T(4,128)S(1)}, f32[4,512]{1,0:T(4,128)}, u32[]{:S(2)}) copy-start(f32[4,512]{1,0:T(4,128)} %geom_ref.1) | copy-start | bytes 24580

commit v5 on v4

--- a/solution.py
+++ b/solution.py
@@ -55,17 +55,44 @@
 
 
 def pack_kernel(
-    count_hbm, place_hbm, basis_ref, signals_hbm, obs_ref, out_ref, count_ref, place_ref, rows_ref, sems
+    count_hbm,
+    place_hbm,
+    basis_hbm,
+    signals_hbm,
+    obs_hbm,
+    out_hbm,
+    count_ref,
+    place_ref,
+    basis_ref,
+    rows_ref,
+    obs_ref,
+    out_ref,
+    sems,
+    out_sems,
 ):
-    small = [
-        pltpu.make_async_copy(count_hbm, count_ref, sems.at[NSIG]),
-        pltpu.make_async_copy(place_hbm, place_ref, sems.at[NSIG + 1]),
+    reads = [
+        pltpu.make_async_copy(src, dst, sems.at[n])
+        for n, (src, dst) in enumerate(
+            [
+                (obs_hbm, obs_ref),
+                (count_hbm, count_ref),
+                (place_hbm, place_ref),
+                (basis_hbm, basis_ref),
+            ]
+            + [(signals_hbm.at[s], rows_ref.at[s]) for s in range(NSIG)]
+        )
     ]
-    large = [
-        pltpu.make_async_copy(signals_hbm.at[s], rows_ref.at[s], sems.at[s]) for s in range(NSIG)
-    ]
-    for copy in small + large:
+    writes = []
+    for n in range(NSIG + 1):
+        rows = slice(n * 16, n * 16 + 16)
+        writes.append(
+            pltpu.make_async_copy(out_ref.at[:, rows, :], out_hbm.at[:, rows, :], out_sems.at[n])
+        )
+    for copy in reads:
         copy.start()
+    for o in range(out_ref.shape[0]):
+        out_ref[o, 0:CHANNELS, :] = jnp.zeros((CHANNELS, PATCH), jnp.bfloat16)
+    reads[0].wait()
     x = obs_ref[...]
     hi = x.astype(jnp.bfloat16).astype(jnp.float32)
     rows = []
@@ -75,11 +102,10 @@
                 rows.append(part[c : c + 1, h * PATCH : (h + 1) * PATCH])
     tail = jnp.concatenate(rows + [jnp.zeros((4, PATCH), jnp.float32)], axis=0)
     for o in range(out_ref.shape[0]):
-        out_ref[o, 0:CHANNELS, :] = jnp.zeros((CHANNELS, PATCH), jnp.bfloat16)
         out_ref[o, OBS_ROW:, :] = tail.astype(jnp.bfloat16)
     row_id = lax.broadcasted_iota(jnp.int32, (16, PATCH), 0)
-    for copy in small:
-        copy.wait()
+    reads[1].wait()
+    reads[2].wait()
     count = count_ref[0, 0]
     for j in range(MAXP):
         place = place_ref[j]
@@ -91,8 +117,10 @@
                 jnp.bfloat16
             )
 
+    writes[NSIG].start()
+    reads[3].wait()
     for s in range(NSIG):
-        large[s].wait()
+        reads[4 + s].wait()
         spec = jnp.dot(
             basis_ref[...], rows_ref[s], preferred_element_type=jnp.float32
         ).astype(jnp.bfloat16)
@@ -103,20 +131,28 @@
                 owner = place_ref[j] // PER_OWN
                 out_ref[owner, s * 16 : s * 16 + 16, :] = spec[:, j * PATCH : (j + 1) * PATCH]
 
+        writes[s].start()
+    for copy in writes:
+        copy.wait()
+
 
 def pack(signals, patch_count, patch_place, obs_pos, owners):
     hbm = pl.BlockSpec(memory_space=pltpu.MemorySpace.HBM)
-    vmem = pl.BlockSpec(memory_space=pltpu.VMEM)
+    shape = (owners, ROWS_MSG, PATCH)
     return pl.pallas_call(
         pack_kernel,
-        in_specs=[hbm, hbm, vmem, hbm, vmem],
-        out_specs=vmem,
-        out_shape=jax.ShapeDtypeStruct((owners, ROWS_MSG, PATCH), jnp.bfloat16),
+        in_specs=[hbm] * 5,
+        out_specs=hbm,
+        out_shape=jax.ShapeDtypeStruct(shape, jnp.bfloat16),
         scratch_shapes=[
             pltpu.SMEM((1, 1), jnp.int32),
             pltpu.SMEM((MAXP,), jnp.int32),
+            pltpu.VMEM((2 * NFREQ, SAMPLES), jnp.bfloat16),
             pltpu.VMEM(signals.shape, signals.dtype),
-            pltpu.SemaphoreType.DMA((NSIG + 2,)),
+            pltpu.VMEM(obs_pos.shape, obs_pos.dtype),
+            pltpu.VMEM(shape, jnp.bfloat16),
+            pltpu.SemaphoreType.DMA((NSIG + 4,)),
+            pltpu.SemaphoreType.DMA((NSIG + 1,)),
         ],
         compiler_params=pltpu.CompilerParams(vmem_limit_bytes=67000000),
         name="pack",
@@ -166,26 +202,25 @@
         acc_ref[m] = part if chunk == 0 else acc_ref[m] + part
 
 
-def finish(t, obs_ref, acc_ref, out_ref):
-    x = [obs_ref[t, c : c + 1, :] for c in range(3)]
-    xx = obs_ref[t, 3:4, :]
+def finish(t, coef_ref, accs, out_ref):
+    coef = coef_ref[t]
     for pair in range(NFREQ // 2):
         lines = ([], [])
         for m in (2 * pair, 2 * pair + 1):
-            total = acc_ref[m]
-            scale = 0.5 * (m + 1) / (16.0 * math.pi**2)
+            terms = accs[m] * coef
+            value = terms[0:8] + terms[8:16]
+            value = value + pltpu.roll(value, 4, axis=0)
+            value = value + pltpu.roll(value, 2, axis=0)
+            value = value * (0.5 * (m + 1) / (16.0 * math.pi**2))
             for part in range(2):
-                row = lambda n: total[2 * n + part : 2 * n + part + 1, :]
-                value = xx * row(0) + row(1) + row(2)
-                value = value + x[0] * (row(3) + row(6)) + x[1] * (row(4) + row(7)) + x[2] * row(5)
-                value = value * scale
-                lines[part].extend([value[:, 0:PATCH], value[:, PATCH:]])
+                row = value[part : part + 1]
+                lines[part].extend([row[:, 0:PATCH], row[:, PATCH:]])
         for part in range(2):
             block = jnp.concatenate(lines[part], axis=0)
             out_ref[part * (NFREQ // 2) + pair, t] = block.astype(out_ref.dtype)
 
 
-def build_observers(arrived_ref, obs_ref):
+def build_observers(arrived_ref, obs_ref, coef_ref):
     for t in range(arrived_ref.shape[0]):
         rows = arrived_ref[t, OBS_ROW : OBS_ROW + 16, :].astype(jnp.float32)
         pos = rows[0:6] + rows[6:12]
@@ -194,7 +229,11 @@
             line = (line - CENTER_X if c == 0 else line) * UNIT
             obs_ref[t, c : c + 1, :] = line
         x = [obs_ref[t, c : c + 1, :] for c in range(3)]
-        obs_ref[t, 3:4, :] = x[0] * x[0] + x[1] * x[1] + x[2] * x[2]
+        xx = x[0] * x[0] + x[1] * x[1] + x[2] * x[2]
+        obs_ref[t, 3:4, :] = xx
+        one = jnp.ones_like(xx)
+        for n, row in enumerate((xx, one, one, x[0], x[1], x[2], x[0], x[1])):
+            coef_ref[t, 2 * n : 2 * n + 2, :] = jnp.broadcast_to(row, (2, OBS_TILE))
 
 
 def build_faces(geom_ref, geo_ref, face_ref):
@@ -275,15 +314,15 @@
 
 
 def pressure_kernel(
-    arrived_ref, geom_ref, out_ref, obs_ref, geo_ref, face_ref, wide_ref, w_ref, acc_ref
+    arrived_ref, geom_ref, out_ref, obs_ref, coef_ref, geo_ref, face_ref, wide_ref, w_ref, acc_ref
 ):
     tiles = arrived_ref.shape[0]
-    build_observers(arrived_ref, obs_ref)
+    build_observers(arrived_ref, obs_ref, coef_ref)
     build_faces(geom_ref, geo_ref, face_ref)
     build_weights(arrived_ref, geo_ref, wide_ref, w_ref)
 
     def tile(t, carry):
-        finish(jnp.maximum(t - 1, 0), obs_ref, acc_ref, out_ref)
+        finish(jnp.maximum(t - 1, 0), coef_ref, acc_ref, out_ref)
         for chunk in range(CHUNKS):
             add_chunk(t, chunk, obs_ref, face_ref, w_ref, acc_ref)
         return carry
@@ -292,7 +331,7 @@
         return tile(2 * i + 1, tile(2 * i, carry))
 
     lax.fori_loop(0, tiles // 2, pair, 0)
-    finish(tiles - 1, obs_ref, acc_ref, out_ref)
+    finish(tiles - 1, coef_ref, acc_ref, out_ref)
 
 
 def partial_pressure(arrived, geom):
@@ -304,6 +343,7 @@
         out_shape=jax.ShapeDtypeStruct((NFREQ, tiles, 4, PATCH), jnp.bfloat16),
         scratch_shapes=[
             pltpu.VMEM((tiles, 8, OBS_TILE), jnp.float32),
+            pltpu.VMEM((tiles, TERMS, OBS_TILE), jnp.float32),
             pltpu.VMEM((8, FACES_OWN), jnp.float32),
             pltpu.VMEM((5, FACES_OWN, PATCH), jnp.float32),
             pltpu.VMEM((4 * FACES_OWN // PATCH, NFREQ * TERMS, PATCH), jnp.float32),

time: 68.1 us -> 67 us (0.984)
  Pallas kernels: 32.3 us -> 31.2 us
where the time goes in v5:
time: 67 us; the launch traced here: 66.7 us
  blocking collectives  34.1 us (51%)
  Pallas kernels  31.2 us (47%)
  between operations  0.68 us (1%)
    pallas_call x1, Pallas kernels, partial_pressure(): pl.pallas_call(pressure_kernel, in_specs=[pl.BlockSpec(memory_space=pltpu...  28.6 us
    all_to_all x1, blocking collectives, local(): lax.all_to_all(outgoing, 'obs', split_axis=0, concat_axis=0, tiled=True)  18.8 us
    all_to_all x1, blocking collectives, local(): lax.all_to_all(out, ('grp', 'obs'), split_axis=0, concat_axis=0, tiled=True)  15.3 us
    pallas_call x1, Pallas kernels, pack(): pl.pallas_call(pack_kernel, in_specs=[hbm] * 5, out_specs=hbm, out_shape=...  2.62 us

profile of v5, /device:TPU:1, one launch (start us, length us, event | category | flops | bytes accessed | tf_op | source)
XLA Modules:
  0.0 66.7 jit_solution(18065437945497063111)
XLA Ops:
  0.0 0.0 copy-start
  0.7 2.6 %pack.1 = bf16[16,80,128]{2,1,0:T(8,128)(2,1)} custom-call(s32[1,1]{1,0:T(1,128)} %bitcast.2.count_hbm, s32[8]{0:T(128)} %place_hbm.1, bf16[16,256]{1,0:T(8,128)(2,1)} %constant.7.basis_hbm, bf16[4,256,1024]{2,1,0:T(8,128)(2,1)} %signals_hbm.1, f32[3,256]{1,0:T(4,128)} %obs_hbm.1), custom_call_target="tpu_custom_call" | custom-call | tf_op jit(solution)/shard_map/pack/pallas_call | solution.py:142
  3.3 18.8 %all_to_all.10.arrived_ref = bf16[16,80,128]{2,1,0:T(8,128)(2,1)S(1)} all-to-all(bf16[16,80,128]{2,1,0:T(8,128)(2,1)} %pack.1), channel_id=1, replica_groups=mesh['grp'=8,'obs'=16] {'obs'}, dimensions={0} | all-to-all | bytes 655360 | tf_op jit(solution)/shard_map/all_to_all | solution.py:362
  22.1 0.0 copy-done
  22.1 28.6 %pressure.1 = bf16[8,16,4,128]{3,2,1,0:T(4,128)(2,1)S(1)} custom-call(bf16[16,80,128]{2,1,0:T(8,128)(2,1)S(1)} %all_to_all.10.arrived_ref, f32[4,512]{1,0:T(4,128)S(1)} %copy-done), custom_call_target="tpu_custom_call" | custom-call | tf_op jit(solution)/shard_map/pressure/pallas_call | solution.py:339
  50.7 15.3 %all_to_all.11 = bf16[128,4,128]{2,1,0:T(4,128)(2,1)S(1)} all-to-all(bf16[128,4,128]{2,1,0:T(4,128)(2,1)S(1)} %bitcast.3), channel_id=1, replica_groups=mesh['grp'=8,'obs'=16] {'grp','obs'}, dimensions={0} | all-to-all | bytes 262144 | tf_op jit(solution)/shard_map/all_to_all | solution.py:365
  66.0 0.1 convert_reduce_fusion
  66.1 0.6 reshape.11
Async XLA Ops:
  0.0 22.1 %copy-start = (f32[4,512]{1,0:T(4,128)S(1)}, f32[4,512]{1,0:T(4,128)}, u32[]{:S(2)}) copy-start(f32[4,512]{1,0:T(4,128)} %geom_ref.1) | copy-start | bytes 24580

commit v6 on v5

--- a/solution.py
+++ b/solution.py
@@ -328,9 +328,11 @@
         return carry
 
     def pair(i, carry):
-        return tile(2 * i + 1, tile(2 * i, carry))
-
-    lax.fori_loop(0, tiles // 2, pair, 0)
+        for n in range(4):
+            carry = tile(4 * i + n, carry)
+        return carry
+
+    lax.fori_loop(0, tiles // 4, pair, 0)
     finish(tiles - 1, coef_ref, acc_ref, out_ref)
 
 

time: 67 us -> 66.5 us (level)
  no operation moved by 1% of the time
where the time goes in v6:
time: 66.5 us; the launch traced here: 66.2 us
  blocking collectives  34.1 us (51%)
  Pallas kernels  30.7 us (46%)
  between operations  0.68 us (1%)
    pallas_call x1, Pallas kernels, partial_pressure(): pl.pallas_call(pressure_kernel, in_specs=[pl.BlockSpec(memory_space=pltpu...  28.1 us
    all_to_all x1, blocking collectives, local(): lax.all_to_all(outgoing, 'obs', split_axis=0, concat_axis=0, tiled=True)  18.8 us
    all_to_all x1, blocking collectives, local(): lax.all_to_all(out, ('grp', 'obs'), split_axis=0, concat_axis=0, tiled=True)  15.3 us
    pallas_call x1, Pallas kernels, pack(): pl.pallas_call(pack_kernel, in_specs=[hbm] * 5, out_specs=hbm, out_shape=...  2.64 us

profile of v6, /device:TPU:1, one launch (start us, length us, event | category | flops | bytes accessed | tf_op | source)
XLA Modules:
  0.0 66.2 jit_solution(13505389455115015226)
XLA Ops:
  0.0 0.0 copy-start
  0.7 2.6 %pack.1 = bf16[16,80,128]{2,1,0:T(8,128)(2,1)} custom-call(s32[1,1]{1,0:T(1,128)} %bitcast.2.count_hbm, s32[8]{0:T(128)} %place_hbm.1, bf16[16,256]{1,0:T(8,128)(2,1)} %constant.7.basis_hbm, bf16[4,256,1024]{2,1,0:T(8,128)(2,1)} %signals_hbm.1, f32[3,256]{1,0:T(4,128)} %obs_hbm.1), custom_call_target="tpu_custom_call" | custom-call | tf_op jit(solution)/shard_map/pack/pallas_call | solution.py:142
  3.3 18.8 %all_to_all.10.arrived_ref = bf16[16,80,128]{2,1,0:T(8,128)(2,1)S(1)} all-to-all(bf16[16,80,128]{2,1,0:T(8,128)(2,1)} %pack.1), channel_id=1, replica_groups=mesh['grp'=8,'obs'=16] {'obs'}, dimensions={0} | all-to-all | bytes 655360 | tf_op jit(solution)/shard_map/all_to_all | solution.py:364
  22.1 0.0 copy-done
  22.1 28.1 %pressure.1 = bf16[8,16,4,128]{3,2,1,0:T(4,128)(2,1)S(1)} custom-call(bf16[16,80,128]{2,1,0:T(8,128)(2,1)S(1)} %all_to_all.10.arrived_ref, f32[4,512]{1,0:T(4,128)S(1)} %copy-done), custom_call_target="tpu_custom_call" | custom-call | tf_op jit(solution)/shard_map/pressure/pallas_call | solution.py:341
  50.2 15.3 %all_to_all.11 = bf16[128,4,128]{2,1,0:T(4,128)(2,1)S(1)} all-to-all(bf16[128,4,128]{2,1,0:T(4,128)(2,1)S(1)} %bitcast.3), channel_id=1, replica_groups=mesh['grp'=8,'obs'=16] {'grp','obs'}, dimensions={0} | all-to-all | bytes 262144 | tf_op jit(solution)/shard_map/all_to_all | solution.py:367
  65.5 0.1 convert_reduce_fusion
  65.6 0.6 reshape.11
Async XLA Ops:
  0.0 22.1 %copy-start = (f32[4,512]{1,0:T(4,128)S(1)}, f32[4,512]{1,0:T(4,128)}, u32[]{:S(2)}) copy-start(f32[4,512]{1,0:T(4,128)} %geom_ref.1) | copy-start | bytes 24580

commit v7 on v6

--- a/solution.py
+++ b/solution.py
@@ -328,11 +328,11 @@
         return carry
 
     def pair(i, carry):
-        for n in range(4):
-            carry = tile(4 * i + n, carry)
+        for n in range(8):
+            carry = tile(8 * i + n, carry)
         return carry
 
-    lax.fori_loop(0, tiles // 4, pair, 0)
+    lax.fori_loop(0, tiles // 8, pair, 0)
     finish(tiles - 1, coef_ref, acc_ref, out_ref)
 
 

time: 66.5 us -> 66.2 us (level)
  no operation moved by 1% of the time
where the time goes in v7:
time: 66.2 us; the launch traced here: 66 us
  blocking collectives  34.1 us (52%)
  Pallas kernels  30.5 us (46%)
  between operations  0.68 us (1%)
    pallas_call x1, Pallas kernels, partial_pressure(): pl.pallas_call(pressure_kernel, in_specs=[pl.BlockSpec(memory_space=pltpu...  27.8 us
    all_to_all x1, blocking collectives, local(): lax.all_to_all(outgoing, 'obs', split_axis=0, concat_axis=0, tiled=True)  18.8 us
    all_to_all x1, blocking collectives, local(): lax.all_to_all(out, ('grp', 'obs'), split_axis=0, concat_axis=0, tiled=True)  15.3 us
    pallas_call x1, Pallas kernels, pack(): pl.pallas_call(pack_kernel, in_specs=[hbm] * 5, out_specs=hbm, out_shape=...  2.63 us

profile of v7, /device:TPU:1, one launch (start us, length us, event | category | flops | bytes accessed | tf_op | source)
XLA Modules:
  0.0 66.0 jit_solution(529412728407468690)
XLA Ops:
  0.0 0.0 copy-start
  0.7 2.6 %pack.1 = bf16[16,80,128]{2,1,0:T(8,128)(2,1)} custom-call(s32[1,1]{1,0:T(1,128)} %bitcast.2.count_hbm, s32[8]{0:T(128)} %place_hbm.1, bf16[16,256]{1,0:T(8,128)(2,1)} %constant.7.basis_hbm, bf16[4,256,1024]{2,1,0:T(8,128)(2,1)} %signals_hbm.1, f32[3,256]{1,0:T(4,128)} %obs_hbm.1), custom_call_target="tpu_custom_call" | custom-call | tf_op jit(solution)/shard_map/pack/pallas_call | solution.py:142
  3.3 18.8 %all_to_all.10.arrived_ref = bf16[16,80,128]{2,1,0:T(8,128)(2,1)S(1)} all-to-all(bf16[16,80,128]{2,1,0:T(8,128)(2,1)} %pack.1), channel_id=1, replica_groups=mesh['grp'=8,'obs'=16] {'obs'}, dimensions={0} | all-to-all | bytes 655360 | tf_op jit(solution)/shard_map/all_to_all | solution.py:364
  22.1 0.0 copy-done
  22.1 27.8 %pressure.1 = bf16[8,16,4,128]{3,2,1,0:T(4,128)(2,1)S(1)} custom-call(bf16[16,80,128]{2,1,0:T(8,128)(2,1)S(1)} %all_to_all.10.arrived_ref, f32[4,512]{1,0:T(4,128)S(1)} %copy-done), custom_call_target="tpu_custom_call" | custom-call | tf_op jit(solution)/shard_map/pressure/pallas_call | solution.py:341
  49.9 15.3 %all_to_all.11 = bf16[128,4,128]{2,1,0:T(4,128)(2,1)S(1)} all-to-all(bf16[128,4,128]{2,1,0:T(4,128)(2,1)S(1)} %bitcast.3), channel_id=1, replica_groups=mesh['grp'=8,'obs'=16] {'grp','obs'}, dimensions={0} | all-to-all | bytes 262144 | tf_op jit(solution)/shard_map/all_to_all | solution.py:367
  65.2 0.1 convert_reduce_fusion
  65.4 0.6 reshape.11
Async XLA Ops:
  0.0 22.1 %copy-start = (f32[4,512]{1,0:T(4,128)S(1)}, f32[4,512]{1,0:T(4,128)}, u32[]{:S(2)}) copy-start(f32[4,512]{1,0:T(4,128)} %geom_ref.1) | copy-start | bytes 24580
